TPU v7x, 32 devices: a whole 2x2x4 slice. The times are simulated.
32 devices in a mesh: stream: 4 (over y, x), replica: 8 (over z, core).
Axes of the slice: x: 2, y: 2, z: 4, core: 2. Of those that a mesh axis runs over, the one named last changes fastest.
Arguments:
- query_embeds: bfloat16 [64, 32, 384], P(('stream', 'replica')), may hold values from -6 to 6
- doc_embeds: bfloat16 [32, 512, 384], P(('stream', 'replica')), may hold values from -6 to 6
- doc_segments: int32 [32, 512], P(('stream', 'replica')), may hold values from 0 to 3, never falling along the last dimension, each value on 1 to 256 neighbouring positions
- candidates: int32 [64, 16], replicated, may hold values from 0 to 127, all different within a row; in each aligned block of 64 rows (0 to 63, 64 to 127, ...) at most 32 rows name the same one
- neg_counts: int32 [64], replicated, may hold values from 1 to 15
- w_qkv: float32 [384, 1152], replicated, may hold values from -0.3125 to 0.3125
- w_out: float32 [384, 384], replicated, may hold values from -1.25 to 1.25
- w_up: float32 [384, 1536], replicated, may hold values from -0.3125 to 0.3125
- w_down: float32 [1536, 384], replicated, may hold values from -0.15625 to 0.15625
- w_head: float32 [384, 96], replicated, may hold values from -0.3125 to 0.3125
- vectors: float32 [5088], replicated, may hold values from -2 to 2, as said below
- mom_qkv: float32 [384, 1152], replicated, may hold values from -6 to 6
- mom_out: float32 [384, 384], replicated, may hold values from -6 to 6
- mom_up: float32 [384, 1536], replicated, may hold values from -6 to 6
- mom_down: float32 [1536, 384], replicated, may hold values from -6 to 6
- mom_head: float32 [384, 96], replicated, may hold values from -6 to 6
- mom_vectors: float32 [5088], replicated, may hold values from -6 to 6
- err_qkv: float32 [8, 384, 1152], P('replica'), may hold values from -3.5 to 3.5
- err_out: float32 [8, 384, 384], P('replica'), may hold values from -3.5 to 3.5
- err_up: float32 [8, 384, 1536], P('replica'), may hold values from -3.5 to 3.5
- err_down: float32 [8, 1536, 384], P('replica'), may hold values from -3.5 to 3.5
- err_head: float32 [8, 384, 96], P('replica'), may hold values from -3.5 to 3.5
- fac_qkv: float32 [1152, 8], replicated, may hold values from -6 to 6
- fac_out: float32 [384, 8], replicated, may hold values from -6 to 6
- fac_up: float32 [1536, 8], replicated, may hold values from -6 to 6
- fac_down: float32 [384, 8], replicated, may hold values from -6 to 6
- fac_head: float32 [96, 8], replicated, may hold values from -6 to 6
Outputs:
- loss: float32 [], replicated
- new_qkv: float32 [384, 1152], replicated
- new_out: float32 [384, 384], replicated
- new_up: float32 [384, 1536], replicated
- new_down: float32 [1536, 384], replicated
- new_head: float32 [384, 96], replicated
- new_vectors: float32 [5088], replicated
- newmom_qkv: float32 [384, 1152], replicated
- newmom_out: float32 [384, 384], replicated
- newmom_up: float32 [384, 1536], replicated
- newmom_down: float32 [1536, 384], replicated
- newmom_head: float32 [384, 96], replicated
- newmom_vectors: float32 [5088], replicated
- newerr_qkv: float32 [8, 384, 1152], P('replica')
- newerr_out: float32 [8, 384, 384], P('replica')
- newerr_up: float32 [8, 384, 1536], P('replica')
- newerr_down: float32 [8, 1536, 384], P('replica')
- newerr_head: float32 [8, 384, 96], P('replica')
- newfac_qkv: float32 [1152, 8], replicated
- newfac_out: float32 [384, 8], replicated
- newfac_up: float32 [1536, 8], replicated
- newfac_down: float32 [384, 8], replicated
- newfac_head: float32 [96, 8], replicated
Inputs may be any that keep to these rules, and one draw needn't show every extreme that they name: `doc_segments`: each row holds all 4 documents in order, each 1 to 256 tokens, one of exactly 256. `candidates`: A query's 16 ids are distinct; no document is named by more than 32 queries, a bound that some block reaches. `vectors`: gains lie near one, biases near zero.
All inputs are finite; a program needn't handle non-finite values.
Results may differ from a plain program's by a relative error of at most 0.0004.
Values may be sent and summed in bfloat16 or wider, within the bound.
No kernel may reach another device: no remote copies, remote signals or barrier semaphores. Data moves between devices by JAX's collectives and lax.ppermute only.
A program may use at most 192 MiB of HBM per device.

v0:
```python
import math

import jax
import jax.numpy as jnp
from jax import lax
from jax.sharding import PartitionSpec as P

D = 384
HEADS = 12
HDIM = 32
FF = 1536
NSEG = 4


HIGH = lax.Precision.HIGHEST
SOFT = 0.03
MOMENTUM = 0.9
RATE = 0.1


def split_vec(packed):
    return jnp.split(
        packed,
        [3 * D, 4 * D, 4 * D + FF, 5 * D + FF, 6 * D + FF, 7 * D + FF, 8 * D + FF, 9 * D + FF],
    )


def inner(first, second):
    return lax.dot_general(
        first, second, (((0,), (0,)), ((), ())), preferred_element_type=jnp.float32
    )


def layer_norm(resid, gain, shift):
    center = resid - jnp.mean(resid, -1, keepdims=True)
    inv_std = lax.rsqrt(jnp.mean(center * center, -1, keepdims=True) + 1e-05)
    normed = center * inv_std
    return (normed * gain + shift, normed, inv_std)


def norm_back(grad_out, gain, normed, inv_std):
    scaled = grad_out * gain
    grad_in = inv_std * (
        scaled
        - jnp.mean(scaled, -1, keepdims=True)
        - normed * jnp.mean(scaled * normed, -1, keepdims=True)
    )
    return (grad_in, jnp.sum(grad_out * normed, 0), jnp.sum(grad_out, 0))


def gelu(value):
    return 0.5 * value * (1.0 + jax.scipy.special.erf(value * 0.7071067811865476))


def gelu_slope(value):
    return (
        0.5 * (1.0 + jax.scipy.special.erf(value * 0.7071067811865476))
        + value * jnp.exp(-0.5 * value * value) * 0.3989422804014327
    )


def rotary(value, cosine, sine):
    half = value.shape[-1] // 2
    return value * cosine + jnp.concatenate([-value[..., half:], value[..., :half]], -1) * sine


def rotary_back(grad, cosine, sine):
    half = grad.shape[-1] // 2
    turned = grad * sine
    return grad * cosine + jnp.concatenate([turned[..., half:], -turned[..., :half]], -1)


def tables(segment):
    count = segment.shape[0]
    places = jnp.arange(count)
    same = segment[:, None] == segment[None, :]
    position = jnp.sum(same & (places[None, :] < places[:, None]), 1).astype(jnp.float32)
    freqs = 10000.0 ** (-(jnp.arange(HDIM // 2).astype(jnp.float32) * 2.0) / HDIM)
    angle = position[:, None] * freqs[None, :]
    cosine = jnp.concatenate([jnp.cos(angle), jnp.cos(angle)], -1)[:, None, :]
    sine = jnp.concatenate([jnp.sin(angle), jnp.sin(angle)], -1)[:, None, :]
    return (same, cosine, sine)


def encode(tokens_in, same, cosine, sine, mats, packed):
    w_qkv, w_out, w_up, w_down, w_head = mats
    b_qkv, b_out, b_up, b_down, gain_one, shift_one, gain_two, shift_two, b_head = split_vec(packed)
    count = tokens_in.shape[0]
    scale = HDIM ** (-0.5)
    qkv = (jnp.dot(tokens_in, w_qkv, preferred_element_type=jnp.float32) + b_qkv).reshape(
        count, 3, HEADS, HDIM
    )
    queries = rotary(qkv[:, 0], cosine, sine).astype(jnp.bfloat16)
    keys_rot = rotary(qkv[:, 1], cosine, sine).astype(jnp.bfloat16)
    values = qkv[:, 2].astype(jnp.bfloat16)
    scores = (
        jnp.einsum("ihd,jhd->hij", queries, keys_rot, preferred_element_type=jnp.float32) * scale
    )
    scores = jnp.where(same[None], scores, -1e30)
    expo = jnp.exp(scores - jnp.max(scores, -1, keepdims=True))
    probs = expo / jnp.sum(expo, -1, keepdims=True)
    probs_low = probs.astype(jnp.bfloat16)
    context = (
        jnp.einsum("hij,jhd->ihd", probs_low, values, preferred_element_type=jnp.float32)
        .reshape(count, D)
        .astype(jnp.bfloat16)
    )
    attended = jnp.dot(context, w_out, preferred_element_type=jnp.float32) + b_out
    hidden_one, normed_one, inv_one = layer_norm(
        tokens_in.astype(jnp.float32) + attended, gain_one, shift_one
    )
    hidden_low = hidden_one.astype(jnp.bfloat16)
    pre_act = jnp.dot(hidden_low, w_up, preferred_element_type=jnp.float32) + b_up
    act_low = gelu(pre_act).astype(jnp.bfloat16)
    mixed = jnp.dot(act_low, w_down, preferred_element_type=jnp.float32) + b_down
    hidden_two, normed_two, inv_two = layer_norm(hidden_one + mixed, gain_two, shift_two)
    second_low = hidden_two.astype(jnp.bfloat16)
    emitted = jnp.dot(second_low, w_head, preferred_element_type=jnp.float32) + b_head
    inv_len = lax.rsqrt(jnp.sum(emitted * emitted, -1, keepdims=True) + 1e-06)
    output = emitted * inv_len
    kept = (
        queries,
        keys_rot,
        values,
        probs,
        probs_low,
        context,
        normed_one,
        inv_one,
        hidden_low,
        pre_act,
        act_low,
        normed_two,
        inv_two,
        second_low,
        inv_len,
        output,
    )
    return (output, kept)


def backward(grad_vec, tokens_in, cosine, sine, kept, mats, packed):
    w_qkv, w_out, w_up, w_down, w_head = mats
    b_qkv, b_out, b_up, b_down, gain_one, shift_one, gain_two, shift_two, b_head = split_vec(packed)
    (
        queries,
        keys_rot,
        values,
        probs,
        probs_low,
        context,
        normed_one,
        inv_one,
        hidden_low,
        pre_act,
        act_low,
        normed_two,
        inv_two,
        second_low,
        inv_len,
        output,
    ) = kept
    count = tokens_in.shape[0]
    scale = HDIM ** (-0.5)
    grad_emit = inv_len * (grad_vec - output * jnp.sum(grad_vec * output, -1, keepdims=True))
    emit_low = grad_emit.astype(jnp.bfloat16)
    grad_head = inner(second_low, emit_low)
    grad_hidden_two = jnp.dot(emit_low, w_head.T, preferred_element_type=jnp.float32)
    grad_resid_two, grad_gain_two, grad_shift_two = norm_back(
        grad_hidden_two, gain_two, normed_two, inv_two
    )
    mixed_low = grad_resid_two.astype(jnp.bfloat16)
    grad_down = inner(act_low, mixed_low)
    grad_act = jnp.dot(mixed_low, w_down.T, preferred_element_type=jnp.float32)
    grad_pre = grad_act * gelu_slope(pre_act)
    pre_low = grad_pre.astype(jnp.bfloat16)
    grad_up = inner(hidden_low, pre_low)
    grad_hidden_one = grad_resid_two + jnp.dot(pre_low, w_up.T, preferred_element_type=jnp.float32)
    grad_resid_one, grad_gain_one, grad_shift_one = norm_back(
        grad_hidden_one, gain_one, normed_one, inv_one
    )
    attn_low = grad_resid_one.astype(jnp.bfloat16)
    grad_out = inner(context, attn_low)
    grad_context = (
        jnp.dot(attn_low, w_out.T, preferred_element_type=jnp.float32)
        .reshape(count, HEADS, HDIM)
        .astype(jnp.bfloat16)
    )
    grad_probs = jnp.einsum(
        "ihd,jhd->hij", grad_context, values, preferred_element_type=jnp.float32
    )
    grad_values = jnp.einsum(
        "hij,ihd->jhd", probs_low, grad_context, preferred_element_type=jnp.float32
    )
    grad_scores = probs * (grad_probs - jnp.sum(grad_probs * probs, -1, keepdims=True))
    scores_low = grad_scores.astype(jnp.bfloat16)
    grad_queries = (
        jnp.einsum("hij,jhd->ihd", scores_low, keys_rot, preferred_element_type=jnp.float32) * scale
    )
    grad_keys = (
        jnp.einsum("hij,ihd->jhd", scores_low, queries, preferred_element_type=jnp.float32) * scale
    )
    grad_queries = rotary_back(grad_queries, cosine, sine)
    grad_keys = rotary_back(grad_keys, cosine, sine)
    grad_qkv_act = jnp.stack([grad_queries, grad_keys, grad_values], 1).reshape(count, 3 * D)
    grad_qkv = inner(tokens_in, grad_qkv_act.astype(jnp.bfloat16))
    grad_packed = jnp.concatenate(
        [
            jnp.sum(grad_qkv_act, 0),
            jnp.sum(grad_resid_one, 0),
            jnp.sum(grad_pre, 0),
            jnp.sum(grad_resid_two, 0),
            grad_gain_one,
            grad_shift_one,
            grad_gain_two,
            grad_shift_two,
            jnp.sum(grad_emit, 0),
        ]
    )
    return (grad_qkv, grad_out, grad_up, grad_down, grad_head, grad_packed)


def cross_entropy(picked, counts, total_queries):
    slots = jnp.arange(picked.shape[1])[None, :]
    logits = jnp.where(slots <= counts[:, None], picked, -1e30)
    peak = jnp.max(logits, -1, keepdims=True)
    expo = jnp.exp(logits - peak)
    total = jnp.sum(expo, -1, keepdims=True)
    losses = peak[:, 0] + jnp.log(total[:, 0]) - logits[:, 0]
    grads = (expo / total - (slots == 0).astype(jnp.float32)) / total_queries
    return (losses, grads)


def orthogonal(left):
    columns = []
    for number in range(left.shape[1]):
        column = left[:, number]
        for before in columns:
            column = column - jnp.sum(before * column) * before
        column = column * lax.rsqrt(jnp.sum(column * column) + 1e-12)
        columns.append(column)
    return jnp.stack(columns, 1)


def shards(
    query_embeds,
    doc_embeds,
    doc_segments,
    candidates,
    neg_counts,
    w_qkv,
    w_out,
    w_up,
    w_down,
    w_head,
    vectors,
    mom_qkv,
    mom_out,
    mom_up,
    mom_down,
    mom_head,
    mom_vectors,
    err_qkv,
    err_out,
    err_up,
    err_down,
    err_head,
    fac_qkv,
    fac_out,
    fac_up,
    fac_down,
    fac_head,
):
    qdev, qlen, width = query_embeds.shape
    row = doc_embeds.shape[1]
    tokens_in = jnp.concatenate([doc_embeds[0], query_embeds.reshape(qdev * qlen, width)], 0)
    segment = jnp.concatenate(
        [doc_segments[0], NSEG + jnp.arange(qdev * qlen, dtype=jnp.int32) // qlen]
    )
    same, cosine, sine = tables(segment)
    weights = (w_qkv, w_out, w_up, w_down, w_head)
    mats = tuple((w.astype(jnp.bfloat16) for w in weights))
    vecs = encode(tokens_in, same, cosine, sine, mats, vectors)[0]
    vec_low = vecs.astype(jnp.bfloat16)
    doc_vecs = vec_low[:row]
    pdim = doc_vecs.shape[1]
    gathered = lax.all_gather(vec_low[row:], ("stream", "replica"), axis=0, tiled=True)
    segmask = doc_segments[0][None, :] == jnp.arange(NSEG)[:, None]
    total_queries = candidates.shape[0]
    my_docs = lax.axis_index(("stream", "replica")) * NSEG + jnp.arange(NSEG)
    owned = (candidates[:, :, None] == my_docs[None, None, :]).astype(jnp.float32)
    query_rows = gathered.reshape(total_queries, qlen, pdim)
    chosen_count = query_rows.shape[0]
    rows_all = chosen_count * qlen
    block_rows = math.gcd(rows_all, 512)
    blocks = query_rows.reshape(rows_all // block_rows, block_rows, pdim)

    def sim_block(rows):
        sim = jnp.dot(rows, doc_vecs.T, preferred_element_type=jnp.float32) / SOFT
        return jnp.where(segmask[None], sim[:, None, :], -1e30)

    def block_total(rows):
        masked = sim_block(rows)
        peak = jnp.max(masked, -1, keepdims=True)
        return peak[..., 0] + jnp.log(jnp.sum(jnp.exp(masked - peak), -1))

    log_total = lax.map(block_total, blocks)
    chosen_scores = (SOFT * log_total).reshape(chosen_count, qlen, NSEG).sum(1)
    table = lax.all_gather(chosen_scores, ("stream", "replica"), axis=1, tiled=True)
    picked = jnp.take_along_axis(table, candidates, 1)
    losses, grad_logits = cross_entropy(picked, neg_counts, total_queries)
    loss = jnp.mean(losses)
    grad_scores = jnp.einsum("qc,qcs->qs", grad_logits, owned)
    token_grads = jnp.repeat(grad_scores, qlen, axis=0).reshape(blocks.shape[0], block_rows, NSEG)

    def back_block(doc_grad, items):
        rows, totals, grads = items
        weight = jnp.exp(sim_block(rows) - totals[..., None])
        sim_low = jnp.einsum("bs,bsu->bu", grads, weight).astype(jnp.bfloat16)
        return (
            doc_grad + inner(sim_low, rows),
            jnp.dot(sim_low, doc_vecs, preferred_element_type=jnp.float32),
        )

    doc_grad, query_grad = lax.scan(
        back_block, jnp.zeros((row, pdim), jnp.float32), (blocks, log_total, token_grads)
    )
    query_grad = query_grad.reshape(chosen_count, qlen * pdim)
    query_local = lax.psum_scatter(
        query_grad.reshape(total_queries * qlen, pdim),
        ("stream", "replica"),
        scatter_dimension=0,
        tiled=True,
    )
    grad_vec = jnp.concatenate([doc_grad, query_local], 0)
    kept = encode(lax.optimization_barrier(tokens_in), same, cosine, sine, mats, vectors)[1]
    grads = backward(grad_vec, tokens_in, cosine, sine, kept, mats, vectors)
    grads = (
        lax.psum(grads[0].astype(jnp.bfloat16), "stream").astype(jnp.float32),
        lax.psum(grads[1].astype(jnp.bfloat16), "stream").astype(jnp.float32),
        lax.psum(grads[2].astype(jnp.bfloat16), "stream").astype(jnp.float32),
        lax.psum(grads[3].astype(jnp.bfloat16), "stream").astype(jnp.float32),
        lax.psum(grads[4].astype(jnp.bfloat16), "stream").astype(jnp.float32),
        lax.psum(grads[5].astype(jnp.bfloat16), "stream").astype(jnp.float32),
    )
    replicas = lax.axis_size("replica")
    devices = lax.axis_size("stream") * replicas
    rate = RATE * qdev * math.sqrt(devices / tokens_in.shape[0])
    errs = (err_qkv, err_out, err_up, err_down, err_head)
    facs = (fac_qkv, fac_out, fac_up, fac_down, fac_head)
    moms = (mom_qkv, mom_out, mom_up, mom_down, mom_head)
    merged = [grads[number] + errs[number][0] for number in range(5)]
    lefts = [jnp.dot(merged[number], facs[number], precision=HIGH) for number in range(5)]
    summed = lax.psum((lefts[0], lefts[1], lefts[2], lefts[3], lefts[4], grads[5]), "replica")
    bases = [orthogonal(summed[number]) for number in range(5)]
    rights_local = [
        lax.dot_general(merged[number], bases[number], (((0,), (0,)), ((), ())), precision=HIGH)
        for number in range(5)
    ]
    rights = lax.psum(
        (rights_local[0], rights_local[1], rights_local[2], rights_local[3], rights_local[4]),
        "replica",
    )
    new_w, new_m, new_e = ([], [], [])
    for number in range(5):
        approx = jnp.dot(bases[number], rights[number].T, precision=HIGH)
        new_e.append((merged[number] - approx / replicas)[None])
        momentum = MOMENTUM * moms[number] + approx
        new_m.append(momentum)
        new_w.append(weights[number] - rate * momentum)
    vec_mom = MOMENTUM * mom_vectors + summed[5]
    new_vec = vectors - rate * vec_mom
    return (
        loss,
        new_w[0],
        new_w[1],
        new_w[2],
        new_w[3],
        new_w[4],
        new_vec,
        new_m[0],
        new_m[1],
        new_m[2],
        new_m[3],
        new_m[4],
        vec_mom,
        new_e[0],
        new_e[1],
        new_e[2],
        new_e[3],
        new_e[4],
        rights[0],
        rights[1],
        rights[2],
        rights[3],
        rights[4],
    )


def solution(mesh):
    return jax.shard_map(
        shards,
        mesh=mesh,
        in_specs=(
            P(("stream", "replica"), None, None),
            P(("stream", "replica"), None, None),
            P(("stream", "replica"), None),
            P(),
            P(),
            P(),
            P(),
            P(),
            P(),
            P(),
            P(),
            P(),
            P(),
            P(),
            P(),
            P(),
            P(),
            P("replica", None, None),
            P("replica", None, None),
            P("replica", None, None),
            P("replica", None, None),
            P("replica", None, None),
            P(),
            P(),
            P(),
            P(),
            P(),
        ),
        out_specs=(
            P(),
            P(),
            P(),
            P(),
            P(),
            P(),
            P(),
            P(),
            P(),
            P(),
            P(),
            P(),
            P(),
            P("replica", None, None),
            P("replica", None, None),
            P("replica", None, None),
            P("replica", None, None),
            P("replica", None, None),
            P(),
            P(),
            P(),
            P(),
            P(),
        ),
        check_vma=False,
    )
```

profile of v0, /device:TPU:0, one launch (start us, length us, event | category | flops | bytes accessed | tf_op | source)
XLA Modules:
  0.0 993.4 jit_solution(15149166866581496086)
XLA Ops:
  20.7 7.4 fusion.83
  28.1 22.1 %fusion.160 = (f32[12,576]{1,0:T(8,128)S(1)}, f32[12,576,576]{1,2,0:T(8,128)}) fusion(f32[12,576,576]{1,2,0:T(8,128)} %fusion.83, pred[576,576]{0,1:T(8,128)(4,1)} %broadcast_compare_fusion), kind=kOutput, calls=%fused_computation.699 | output fusion | flops 23888448 | bytes 32209920 | tf_op jit(solution)/shard_map/sub | solution.py:100
  50.2 7.6 fusion.58
  59.7 4.5 fusion.162
  67.0 45.4 %all_gather.6 = bf16[2048,96]{1,0:T(8,128)(2,1)S(1)} all-gather(bf16[64,96]{1,0:T(8,128)(2,1)S(1)} %copy.138), channel_id=1, replica_groups=mesh['stream'=4,'replica'=8] {'stream','replica'}, dimensions={0}, use_global_device_ids=true | all-gather | bytes 405504 | tf_op jit(solution)/shard_map/all_gather | solution.py:287
  112.4 11.2 %while.24 = (s32[]{:T(128)}, f32[4,512,4]{1,2,0:T(4,128)}, bf16[4,512,96]{2,1,0:T(8,128)(2,1)S(1)}, bf16[512,96]{1,0:T(8,128)(2,1)S(1)}, s32[512]{0:T(512)S(1)}, /*index=5*/s32[]{:T(128)}) while((s32[]{:T(128)}, f32[4,512,4]{1,2,0:T(4,128)}, bf16[4,512,96]{2,1,0:T(8,128)(2,1)S(1)}, bf16[512,96]{1,0:T(8,128)(2,1)S(1)}, ...), condition=%wide.region_11.12_spmd.clone, body=%wide.region_8.11_spmd.clone.sunk | while | flops 55836672 | bytes 3465301 | solution.py:307
  124.6 36.9 %all-gather = f32[32,4,64]{2,1,0:T(4,128)S(1)} all-gather(f32[1,4,64]{2,1,0:T(4,128)S(1)} %bitcast.242), channel_id=1, replica_groups=mesh['stream'=4,'replica'=8] {'stream','replica'}, dimensions={0}, use_global_device_ids=true | all-gather | bytes 33792 | tf_op jit(solution)/shard_map/all_gather | solution.py:309
  161.5 7.3 gather_fusion
  170.5 29.0 %while.25 = (s32[]{:T(128)}, f32[512,96]{0,1:T(8,128)S(1)}, f32[4,512,96]{1,2,0:T(8,128)}, bf16[4,512,4]{1,0,2:T(4,128)(2,1)S(1)}, bf16[4,512,96]{2,1,0:T(8,128)...) while((s32[]{:T(128)}, f32[512,96]{0,1:T(8,128)S(1)}, ...), condition=%wide.region_24.25_spmd.clone, body=%wide.region_23.24_spmd.clone.sunk | while | flops 155551744 | bytes 5351563 | solution.py:325
  214.3 11.2 %fusion.167 = (f32[12,576]{1,0:T(8,128)S(1)}, f32[12,576,576]{1,2,0:T(8,128)}) fusion(pred[576,576]{0,1:T(8,128)(4,1)} %broadcast_compare_fusion, bf16[576,12,32]{0,2,1:T(8,128)(2,1)} %get-tuple-element.599, bf16[576,12,32]{0,2,1:T(8,128)(2,1)S(1)} %get-tuple-element.598), kind=kOutput, calls=%fused_computation.702 | convolution fusion | flops 270729792 | bytes 17169408 | tf_op jit(solution)/shard_map/sub | solution.py:100
  225.6 8.0 fusion.55
  241.8 94.5 %reduce-scatter.4.cloned.1.call-done = f32[64,96]{1,0:T(8,128)} async-done(((f32[2048,96]{1,0:T(8,128)}), f32[64,96]{1,0:T(8,128)}) %reduce-scatter.4.cloned.1.call-update) | async-done | bytes 24592
  359.1 7.4 fusion.48
  366.5 12.1 %multiply_reduce_fusion = (f32[12,576]{1,0:T(8,128)S(1)}, f32[12,576,576]{1,2,0:T(8,128)}) fusion(f32[12,576,576]{1,2,0:T(8,128)} %get-tuple-element.646, f32[12,576]{1,0:T(8,128)S(1)} %copy-done.75, bf16[576,12,32]{0,2,1:T(8,128)(2,1)S(1)} %bitcast.231, f32[576,3,12,32]{0,3,2,1:T(8,128)} %bitcast.216), kind=kOutput, calls=%fused_computation.40 | convolution fusion | flops 266740992 | bytes 34609152 | tf_op jit(solution)/shard_map/ihd,jhd->hij/dot_general | solution.py:189
  378.7 12.0 %multiply_convert_fusion = bf16[12,576,576]{1,2,0:T(8,128)(2,1)S(1)} fusion(f32[12,576,576]{1,2,0:T(8,128)} %get-tuple-element.658, f32[12,576]{1,0:T(8,128)S(1)} %get-tuple-element.657, f32[12,576,576]{1,2,0:T(8,128)} %get-tuple-element.646, f32[12,576]{1,0:T(8,128)S(1)} %copy-done.75), kind=kLoop, calls=%fused_computation.39 | loop fusion | flops 15925248 | bytes 39868416 | tf_op jit(solution)/shard_map/convert_element_type | solution.py:196
  401.3 89.7 %all-reduce.9.cloned.1.call-done = (bf16[384,1152]{1,0:T(8,128)(2,1)}, bf16[384,384]{1,0:T(8,128)(2,1)}, bf16[384,1536]{1,0:T(8,128)(2,1)}, bf16[1536,384]{1,0:T(8,128)(2,1)}, bf16[384,96]{0,1:T(8,128)(2,1)}) async-done(((bf16[384,1152]{1,0:T(8,128)(2,1)}, bf16[384,384]{1,0:T(8,128)(2,1)}, bf16[384,1536]{1,0:T(8,128)(2,1)}, bf16[1536,384]{1,0:T(8,128)(2,1)}, bf16[384,96]{0,1:T(8,128)(2,1)}), ...) | async-done | bytes 3612688 | tf_op jit(solution)/shard_map/psum | solution.py:339
  497.2 4.4 fusion.70
  519.9 16.5 %psum.134 = bf16[5088]{0:T(1024)(128)(2,1)} all-reduce(bf16[5088]{0:T(1024)(128)(2,1)} %dynamic-update-slice.8), channel_id=1, replica_groups=mesh['stream'=4,'replica'=8] {'stream'}, use_global_device_ids=true, to_apply=%region_236.237 | all-reduce | flops 5088 | bytes 20352 | tf_op jit(solution)/shard_map/psum | solution.py:344
  536.5 22.3 %all-reduce.7.cloned.1.call-done = (f32[384,8]{0,1:T(8,128)}, f32[384,8]{0,1:T(8,128)}, f32[384,8]{0,1:T(8,128)}, f32[1536,8]{0,1:T(8,128)}, f32[384,8]{0,1:T(8,128)}) async-done(((f32[384,8]{0,1:T(8,128)}, f32[384,8]{0,1:T(8,128)}, f32[384,8]{0,1:T(8,128)}, f32[1536,8]{0,1:T(8,128)}, f32[384,8]{0,1:T(8,128)}), (f32[384,8]{0,1:T(8,128)}, f32[384,8]{0,1:T(8,128)}, f32[384,8]{0,1:T(8,128)}, ...) | async-done | bytes 98320 | tf_op jit(solution)/shard_map/psum | solution.py:354
  566.3 5.9 multiply_reduce_fusion.161
  578.6 7.1 multiply_reduce_fusion.160
  586.4 4.6 multiply_reduce_fusion.159
  596.7 4.4 multiply_reduce_fusion.158
  619.6 5.9 multiply_reduce_fusion.126
  631.9 6.9 multiply_reduce_fusion.125
  639.4 4.5 multiply_reduce_fusion.124
  649.6 4.4 multiply_reduce_fusion.123
  664.9 19.1 %subtract_multiply_fusion.27 = (f32[384,1]{0,1:T(1,128)S(1)}, f32[384,1]{0,1:T(1,128)S(1)}, f32[384,1]{0,1:T(1,128)S(1)}, f32[384,1]{0,1:T(1,128)S(1)}, f32[384,...) fusion(f32[384,1]{0,1:T(1,128)} %get-tuple-element.565, f32[384,8]{0,1:T(8,128)} %get-tuple-element.420, ...), kind=kLoop, calls=%fused_computation.596 | loop fusion | flops 24192 | bytes 23180 | tf_op jit(solution)/shard_map/mul | solution.py:240
  694.6 5.8 multiply_reduce_fusion.91
  706.8 7.5 multiply_reduce_fusion.90
  715.0 4.4 multiply_reduce_fusion.89
  725.2 5.0 multiply_reduce_fusion.88
  750.8 5.9 multiply_reduce_fusion.56
  763.1 7.6 multiply_reduce_fusion.55
  771.4 4.4 multiply_reduce_fusion.54
  781.5 5.1 multiply_reduce_fusion.53
  799.7 19.2 %subtract_multiply_fusion.13 = (f32[384,1]{0,1:T(1,128)S(1)}, f32[384,1]{0,1:T(1,128)S(1)}, f32[384,1]{0,1:T(1,128)S(1)}, f32[384,1]{0,1:T(1,128)}, f32[384,1]{0...) fusion(f32[384,1]{0,1:T(1,128)} %get-tuple-element.476, f32[384,8]{0,1:T(8,128)} %get-tuple-element.423, f32[]{:T(128)S(6)} %rsqrt.213, ...), kind=kLoop, calls=%fused_computation.580 | loop fusion | flops 24192 | bytes 23180 | tf_op jit(solution)/shard_map/mul | solution.py:240
  819.9 18.4 %subtract_multiply_fusion.34 = (f32[384,1]{0,1:T(1,128)S(1)}, f32[384,1]{0,1:T(1,128)S(1)}, f32[384,1]{0,1:T(1,128)S(1)}, f32[384,1]{0,1:T(1,128)S(1)}, f32[384,...) fusion(f32[384,1]{0,1:T(1,128)} %get-tuple-element.595, f32[384,8]{0,1:T(8,128)S(1)} %copy-done.73, ...), kind=kLoop, calls=%fused_computation.604 | loop fusion | flops 24192 | bytes 23180 | tf_op jit(solution)/shard_map/mul | solution.py:240
  841.6 18.4 %subtract_multiply_fusion.20 = (f32[384,1]{0,1:T(1,128)S(1)}, f32[384,1]{0,1:T(1,128)S(1)}, f32[384,1]{0,1:T(1,128)S(1)}, f32[384,1]{0,1:T(1,128)S(1)}, f32[384,...) fusion(f32[384,1]{0,1:T(1,128)S(1)} %copy-done.100, f32[384,8]{0,1:T(8,128)} %get-tuple-element.421, ...), kind=kLoop, calls=%fused_computation.588 | loop fusion | flops 24192 | bytes 23180 | tf_op jit(solution)/shard_map/mul | solution.py:240
  860.0 4.1 fusion.69
  868.1 5.2 multiply_reduce_fusion.20
  877.8 6.5 multiply_reduce_fusion.19
  892.0 5.1 multiply_reduce_fusion.17
  907.3 17.9 %subtract_multiply_fusion.6 = (f32[1536,1]{0,1:T(1,128)S(1)}, f32[1536,1]{0,1:T(1,128)S(1)}, f32[1536,1]{0,1:T(1,128)S(1)}, f32[1536,1]{0,1:T(1,128)S(1)}, f32[1...) fusion(f32[1536,1]{0,1:T(1,128)S(1)} %get-tuple-element.505, f32[1536,8]{0,1:T(8,128)S(1)} %copy-done.63, ...), kind=kLoop, calls=%fused_computation.297 | loop fusion | flops 96768 | bytes 92300 | tf_op jit(solution)/shard_map/mul | solution.py:240
  929.3 31.7 %all-reduce.10 = (f32[1152,8]{0,1:T(8,128)}, f32[384,8]{0,1:T(8,128)}, f32[1536,8]{0,1:T(8,128)}, f32[384,8]{0,1:T(8,128)}, f32[96,8]{0,1:T(8,128)}, /*index=5*/f32[5088]{0:T(1024)}) all-reduce(f32[1152,8]{0,1:T(8,128)S(1)} %fusion.79, f32[384,8]{0,1:T(8,128)} %fusion.107, ...), channel_id=1, replica_groups=mesh['stream'=4,'replica'=8] {'replica'}, use_global_device_ids=true, to_apply=%region_70.71 | all-reduce | flops 33504 | bytes 257856 | tf_op jit(solution)/shard_map/psum | solution.py:360
  968.0 6.0 multiply_subtract_fusion.2
  974.1 4.9 multiply_subtract_fusion
  979.6 5.7 multiply_subtract_fusion.1
  (487 shorter events, 287.2 us)
Async XLA Ops:
  7.2 490.0 %copy-start = (f32[1536,8]{0,1:T(8,128)S(1)}, f32[1536,8]{0,1:T(8,128)}, u32[]{:S(2)}) copy-start(f32[1536,8]{0,1:T(8,128)} %param.55) | copy-start | bytes 147460
  7.2 329.0 %reduce-scatter.4.cloned.1.call-start = ((), (), s32[]{:S(2)}) async-start(), calls=%async_computation.1 | async-start | bytes 1081344
  8.5 55.9 %copy-start.114 = (f32[96]{0:T(128)}, f32[96]{0:T(128)S(1)}, u32[]{:S(2)}) copy-start(f32[96]{0:T(128)S(1)} %split.46) | copy-start | bytes 1156
  9.2 50.2 %copy-start.88 = (f32[1536]{0:T(1024)}, f32[1536]{0:T(1024)S(1)}, u32[]{:S(2)}) copy-start(f32[1536]{0:T(1024)S(1)} %split.42) | copy-start | bytes 18436
  10.7 47.2 %copy-start.98 = (f32[384]{0:T(512)}, f32[384]{0:T(512)S(1)}, u32[]{:S(2)}) copy-start(f32[384]{0:T(512)S(1)} %get-tuple-element.634) | copy-start | bytes 4612
  10.7 48.7 %copy-start.90 = (f32[384]{0:T(512)}, f32[384]{0:T(512)S(1)}, u32[]{:S(2)}) copy-start(f32[384]{0:T(512)S(1)} %get-tuple-element.633) | copy-start | bytes 4612
  10.7 48.7 %copy-start.106 = (f32[384]{0:T(512)}, f32[384]{0:T(512)S(1)}, u32[]{:S(2)}) copy-start(f32[384]{0:T(512)S(1)} %get-tuple-element.632) | copy-start | bytes 4612
  10.8 48.7 %copy-start.112 = (f32[384]{0:T(512)}, f32[384]{0:T(512)S(1)}, u32[]{:S(2)}) copy-start(f32[384]{0:T(512)S(1)} %get-tuple-element.631) | copy-start | bytes 4612
  10.8 53.7 %copy-start.86 = (f32[384]{0:T(512)}, f32[384]{0:T(512)S(1)}, u32[]{:S(2)}) copy-start(f32[384]{0:T(512)S(1)} %get-tuple-element.629) | copy-start | bytes 4612
  10.8 53.7 %copy-start.92 = (f32[384]{0:T(512)}, f32[384]{0:T(512)S(1)}, u32[]{:S(2)}) copy-start(f32[384]{0:T(512)S(1)} %get-tuple-element.630) | copy-start | bytes 4612
  50.2 7.7 copy-start.13
  50.2 7.7 copy-start.28
  50.2 7.7 copy-start.57
  64.1 48.2 %copy-start.61 = (s32[1,512]{1,0:T(1,128)S(1)}, s32[1,512]{1,0:T(1,128)}, u32[]{:S(2)}) copy-start(s32[1,512]{1,0:T(1,128)} %param.33) | copy-start | bytes 6148
  161.5 7.7 copy-start.117
  161.5 9.0 copy-start.62
  202.0 289.0 %all-reduce.9.cloned.1.call-start = ((), (), s32[]{:S(2)}) async-start(), calls=%async_computation.3 | async-start | bytes 7225344 | tf_op jit(solution)/shard_map/psum | solution.py:339
  214.3 11.2 %copy-start.25 = (bf16[576,12,32]{0,2,1:T(8,128)(2,1)}, bf16[576,12,32]{0,2,1:T(8,128)(2,1)S(1)}, u32[]{:S(2)}) copy-start(bf16[576,12,32]{0,2,1:T(8,128)(2,1)S(1)} %get-tuple-element.598) | copy-start | bytes 1327108
  225.5 8.0 copy-start.74
  225.5 8.1 copy-start.14
  225.5 8.1 copy-start.23
  225.5 8.1 copy-start.99
  366.5 29.7 %copy-start.27 = (f32[576,1,12,32]{0,3,2,1:T(8,128)}, f32[576,1,12,32]{0,3,2,1:T(8,128)S(1)}, u32[]{:S(2)}) copy-start(f32[576,1,12,32]{0,3,2,1:T(8,128)S(1)} %fusion.48) | copy-start | bytes 2654212
  378.7 12.0 %copy-start.40 = (bf16[576,12,32]{0,2,1:T(8,128)(2,1)S(1)}, bf16[576,12,32]{0,2,1:T(8,128)(2,1)}, u32[]{:S(2)}) copy-start(bf16[576,12,32]{0,2,1:T(8,128)(2,1)} %get-tuple-element.599) | copy-start | bytes 1327108
  399.3 91.7 %copy-start.7 = (f32[1,384,1152]{2,1,0:T(8,128)S(1)}, f32[1,384,1152]{2,1,0:T(8,128)}, u32[]{:S(2)}) copy-start(f32[1,384,1152]{2,1,0:T(8,128)} %param.48) | copy-start | bytes 5308420
  399.3 91.7 %copy-start.77 = (f32[1152,8]{0,1:T(8,128)S(1)}, f32[1152,8]{0,1:T(8,128)}, u32[]{:S(2)}) copy-start(f32[1152,8]{0,1:T(8,128)} %param.53) | copy-start | bytes 110596
  399.3 95.3 %copy-start.101 = (f32[384,8]{0,1:T(8,128)S(1)}, f32[384,8]{0,1:T(8,128)}, u32[]{:S(2)}) copy-start(f32[384,8]{0,1:T(8,128)} %param.54) | copy-start | bytes 36868
  399.4 159.4 %all-reduce.7.cloned.1.call-start = ((), (), s32[]{:S(2)}) async-start(), calls=%async_computation.2 | async-start | bytes 196608 | tf_op jit(solution)/shard_map/psum | solution.py:354
  494.6 7.8 copy-start.1
  494.6 7.8 copy-start.11
  494.7 7.8 copy-start.103
  507.0 312.6 %copy-start.54 = (bf16[384,96]{0,1:T(8,128)(2,1)S(1)}, bf16[384,96]{0,1:T(8,128)(2,1)}, u32[]{:S(2)}) copy-start(bf16[384,96]{0,1:T(8,128)(2,1)} %get-tuple-element.428) | copy-start | bytes 221188
  507.0 331.9 %copy-start.18 = (bf16[384,1152]{1,0:T(8,128)(2,1)S(1)}, bf16[384,1152]{1,0:T(8,128)(2,1)}, u32[]{:S(2)}) copy-start(bf16[384,1152]{1,0:T(8,128)(2,1)} %get-tuple-element.424) | copy-start | bytes 2654212
  558.8 261.1 %copy-start.73 = (f32[384,8]{0,1:T(8,128)S(1)}, f32[384,8]{0,1:T(8,128)}, u32[]{:S(2)}) copy-start(f32[384,8]{0,1:T(8,128)} %get-tuple-element.419) | copy-start | bytes 36868
  560.4 15.6 %copy-start.82 = (f32[384]{0:T(512)}, f32[384]{0:T(512)S(1)}, u32[]{:S(2)}) copy-start(f32[384]{0:T(512)S(1)} %get-tuple-element.260) | copy-start | bytes 4612
  613.6 15.7 %copy-start.83 = (f32[384]{0:T(512)}, f32[384]{0:T(512)S(1)}, u32[]{:S(2)}) copy-start(f32[384]{0:T(512)S(1)} %get-tuple-element.252) | copy-start | bytes 4612
  684.7 134.2 %copy-start.67 = (f32[384,8]{0,1:T(8,128)}, f32[384,8]{0,1:T(8,128)S(1)}, u32[]{:S(2)}) copy-start(f32[384,8]{0,1:T(8,128)S(1)} %stack.23) | copy-start | bytes 36868
  688.6 15.7 %copy-start.78 = (f32[384]{0:T(512)}, f32[384]{0:T(512)S(1)}, u32[]{:S(2)}) copy-start(f32[384]{0:T(512)S(1)} %get-tuple-element.241) | copy-start | bytes 4612
  744.7 15.7 %copy-start.80 = (f32[384]{0:T(512)}, f32[384]{0:T(512)S(1)}, u32[]{:S(2)}) copy-start(f32[384]{0:T(512)S(1)} %get-tuple-element.233) | copy-start | bytes 4612
  763.1 7.7 copy-start.97
  797.8 43.8 %copy-start.100 = (f32[384,1]{0,1:T(1,128)S(1)}, f32[384,1]{0,1:T(1,128)}, u32[]{:S(2)}) copy-start(f32[384,1]{0,1:T(1,128)} %get-tuple-element.535) | copy-start | bytes 4612
  819.7 44.4 %copy-start.66 = (f32[384,8]{0,1:T(8,128)}, f32[384,8]{0,1:T(8,128)S(1)}, u32[]{:S(2)}) copy-start(f32[384,8]{0,1:T(8,128)S(1)} %stack.26) | copy-start | bytes 36868
  839.0 25.1 %copy-start.64 = (f32[384,8]{0,1:T(8,128)}, f32[384,8]{0,1:T(8,128)S(1)}, u32[]{:S(2)}) copy-start(f32[384,8]{0,1:T(8,128)S(1)} %stack.22) | copy-start | bytes 36868
  841.6 22.5 %copy-start.63 = (f32[1536,8]{0,1:T(8,128)S(1)}, f32[1536,8]{0,1:T(8,128)}, u32[]{:S(2)}) copy-start(f32[1536,8]{0,1:T(8,128)} %get-tuple-element.422) | copy-start | bytes 147460
  868.1 94.2 %copy-start.46 = (f32[384,96]{0,1:T(8,128)S(1)}, f32[384,96]{0,1:T(8,128)}, u32[]{:S(2)}) copy-start(f32[384,96]{0,1:T(8,128)} %param.40) | copy-start | bytes 442372
  868.1 94.2 %copy-start.55 = (bf16[384,96]{0,1:T(8,128)(2,1)S(1)}, bf16[384,96]{0,1:T(8,128)(2,1)}, u32[]{:S(2)}) copy-start(bf16[384,96]{0,1:T(8,128)(2,1)} %get-tuple-element.428) | copy-start | bytes 221188
  925.9 38.8 %copy-start.16 = (f32[384,384]{1,0:T(8,128)S(1)}, f32[384,384]{1,0:T(8,128)}, u32[]{:S(2)}) copy-start(f32[384,384]{1,0:T(8,128)} %param.37) | copy-start | bytes 1769476
  925.9 38.8 %copy-start.34 = (bf16[384,384]{1,0:T(8,128)(2,1)S(1)}, bf16[384,384]{1,0:T(8,128)(2,1)}, u32[]{:S(2)}) copy-start(bf16[384,384]{1,0:T(8,128)(2,1)} %get-tuple-element.425) | copy-start | bytes 884740
  (73 other events, 284.5 us)
Sparse Core Ops, SparseCore 0:
  202.1 134.0 reduce-scatter.3
  399.5 91.4 all-reduce.8
  505.4 53.2 all-reduce.6
where the time goes:
time: 1010 us; the launch traced here: 993 us
  other arithmetic  388 us (38%)
  waiting for transfers between devices  207 us (20%)
  matrix products  165 us (16%)
  blocking collectives  130 us (13%)
  local copies, waits for them, and re-layouts  58 us (6%)
  between operations  44.8 us (4%)
    reduce_sum x49, other arithmetic, orthogonal(): column = column - jnp.sum(before * column) * before  174 us
    mul x10, other arithmetic, orthogonal(): column = column * lax.rsqrt(jnp.sum(column * column) + 1e-12)  98 us
    unnamed x4, waiting for transfers between devices  94.5 us
    psum x1, waiting for transfers between devices, shards(): lax.psum(grads[0].astype(jnp.bfloat16), 'stream').astype(jnp.float32)  89.7 us
    reduce_sum x21, other arithmetic, orthogonal(): column = column * lax.rsqrt(jnp.sum(column * column) + 1e-12)  47.6 us
    all_gather x1, blocking collectives, shards(): lax.all_gather(vec_low[row:], ('stream', 'replica'), axis=0, tiled=True)  45.4 us
    all_gather x1, blocking collectives, shards(): lax.all_gather(chosen_scores, ('stream', 'replica'), axis=1, tiled=True)  36.9 us
    psum x1, blocking collectives, shards(): lax.psum((rights_local[0], rights_local[1], rights_local[2], rights_local...  31.7 us
  transfers between devices with their start and end apart: 3, of which 3 were waited for; matrix products, arithmetic and copies ran while one was open for 5% of the time, Pallas kernels for 0%

commit v1 on v0

--- a/solution.py
+++ b/solution.py
@@ -3,6 +3,7 @@
 import jax
 import jax.numpy as jnp
 from jax import lax
+from jax.experimental import pallas as pl
 from jax.sharding import PartitionSpec as P
 
 D = 384
@@ -164,23 +165,19 @@
     scale = HDIM ** (-0.5)
     grad_emit = inv_len * (grad_vec - output * jnp.sum(grad_vec * output, -1, keepdims=True))
     emit_low = grad_emit.astype(jnp.bfloat16)
-    grad_head = inner(second_low, emit_low)
     grad_hidden_two = jnp.dot(emit_low, w_head.T, preferred_element_type=jnp.float32)
     grad_resid_two, grad_gain_two, grad_shift_two = norm_back(
         grad_hidden_two, gain_two, normed_two, inv_two
     )
     mixed_low = grad_resid_two.astype(jnp.bfloat16)
-    grad_down = inner(act_low, mixed_low)
     grad_act = jnp.dot(mixed_low, w_down.T, preferred_element_type=jnp.float32)
     grad_pre = grad_act * gelu_slope(pre_act)
     pre_low = grad_pre.astype(jnp.bfloat16)
-    grad_up = inner(hidden_low, pre_low)
     grad_hidden_one = grad_resid_two + jnp.dot(pre_low, w_up.T, preferred_element_type=jnp.float32)
     grad_resid_one, grad_gain_one, grad_shift_one = norm_back(
         grad_hidden_one, gain_one, normed_one, inv_one
     )
     attn_low = grad_resid_one.astype(jnp.bfloat16)
-    grad_out = inner(context, attn_low)
     grad_context = (
         jnp.dot(attn_low, w_out.T, preferred_element_type=jnp.float32)
         .reshape(count, HEADS, HDIM)
@@ -203,7 +200,6 @@
     grad_queries = rotary_back(grad_queries, cosine, sine)
     grad_keys = rotary_back(grad_keys, cosine, sine)
     grad_qkv_act = jnp.stack([grad_queries, grad_keys, grad_values], 1).reshape(count, 3 * D)
-    grad_qkv = inner(tokens_in, grad_qkv_act.astype(jnp.bfloat16))
     grad_packed = jnp.concatenate(
         [
             jnp.sum(grad_qkv_act, 0),
@@ -217,29 +213,76 @@
             jnp.sum(grad_emit, 0),
         ]
     )
-    return (grad_qkv, grad_out, grad_up, grad_down, grad_head, grad_packed)
-
-
-def cross_entropy(picked, counts, total_queries):
-    slots = jnp.arange(picked.shape[1])[None, :]
-    logits = jnp.where(slots <= counts[:, None], picked, -1e30)
-    peak = jnp.max(logits, -1, keepdims=True)
-    expo = jnp.exp(logits - peak)
-    total = jnp.sum(expo, -1, keepdims=True)
-    losses = peak[:, 0] + jnp.log(total[:, 0]) - logits[:, 0]
-    grads = (expo / total - (slots == 0).astype(jnp.float32)) / total_queries
-    return (losses, grads)
-
-
-def orthogonal(left):
-    columns = []
-    for number in range(left.shape[1]):
-        column = left[:, number]
-        for before in columns:
-            column = column - jnp.sum(before * column) * before
-        column = column * lax.rsqrt(jnp.sum(column * column) + 1e-12)
-        columns.append(column)
-    return jnp.stack(columns, 1)
+    pairs = (
+        (tokens_in, grad_qkv_act.astype(jnp.bfloat16)),
+        (context, attn_low),
+        (hidden_low, pre_low),
+        (act_low, mixed_low),
+        (second_low, emit_low),
+    )
+    return (pairs, grad_packed)
+
+
+def peers(number):
+    return [[(i, i ^ k) for i in range(number)] for k in range(number)]
+
+
+def spread(value, axis):
+    turns = peers(lax.axis_size(axis))
+    return jnp.stack([value] + [lax.ppermute(value, axis, turn) for turn in turns[1:]], 0)
+
+
+def fold(value, axis):
+    turns = peers(lax.axis_size(axis))
+    total = value[0]
+    for k, turn in enumerate(turns):
+        if k:
+            total = total + lax.ppermute(value[k], axis, turn)
+    return total
+
+
+def all_sum(value):
+    axes = ("stream", "replica")
+    count = lax.axis_size("stream") * lax.axis_size("replica")
+    rows, cols = value.shape
+    pieces = value.reshape(rows, count, cols // count).transpose(1, 0, 2)
+    got = lax.all_to_all(pieces, axes, 0, 0, tiled=True)
+    mine = jnp.sum(got, 0)
+    back = lax.all_to_all(
+        jnp.broadcast_to(mine[None], pieces.shape), axes, 0, 0, tiled=True
+    )
+    return back.transpose(1, 0, 2).reshape(rows, cols)
+
+
+def thirds(value):
+    high = lax.reduce_precision(value, 8, 7)
+    rest = value - high
+    mid = lax.reduce_precision(rest, 8, 7)
+    low = rest - mid
+    return [part.astype(jnp.bfloat16) for part in (high, mid, low)]
+
+
+def exact(left, right, contract):
+    out = lax.dot_general(
+        jnp.concatenate(thirds(left), 0), right, (contract, ((), ())),
+        preferred_element_type=jnp.float32,
+    )
+    return out[:8] + out[8:16] + out[16:]
+
+
+def basis_kernel(bounds, left_ref, out_ref):
+    blocks = [left_ref[:, lo:hi] for lo, hi in bounds]
+    places = lax.broadcasted_iota(jnp.int32, (8, 1), 0)
+    for turn in range(8):
+        for n, block in enumerate(blocks):
+            row = block[turn : turn + 1]
+            row = row * lax.rsqrt(jnp.sum(row * row, -1, keepdims=True) + 1e-12)
+            shares = jnp.sum(block * row, -1, keepdims=True)
+            shares = jnp.where(places > turn, shares, 0.0)
+            block = block - shares * row
+            blocks[n] = jnp.where(places == turn, row, block)
+    for (lo, hi), block in zip(bounds, blocks):
+        out_ref[:, lo:hi] = block
 
 
 def shards(
@@ -271,129 +314,149 @@
     fac_down,
     fac_head,
 ):
+    streams, replicas = lax.axis_size("stream"), lax.axis_size("replica")
+    devices = streams * replicas
+    my_stream, my_replica = lax.axis_index("stream"), lax.axis_index("replica")
     qdev, qlen, width = query_embeds.shape
     row = doc_embeds.shape[1]
-    tokens_in = jnp.concatenate([doc_embeds[0], query_embeds.reshape(qdev * qlen, width)], 0)
-    segment = jnp.concatenate(
-        [doc_segments[0], NSEG + jnp.arange(qdev * qlen, dtype=jnp.int32) // qlen]
-    )
-    same, cosine, sine = tables(segment)
+    qtok = qdev * qlen
     weights = (w_qkv, w_out, w_up, w_down, w_head)
+    moms = (mom_qkv, mom_out, mom_up, mom_down, mom_head)
+    errs = (err_qkv[0], err_out[0], err_up[0], err_down[0], err_head[0])
+    facs = (fac_qkv, fac_out, fac_up, fac_down, fac_head)
     mats = tuple((w.astype(jnp.bfloat16) for w in weights))
-    vecs = encode(tokens_in, same, cosine, sine, mats, vectors)[0]
-    vec_low = vecs.astype(jnp.bfloat16)
-    doc_vecs = vec_low[:row]
-    pdim = doc_vecs.shape[1]
-    gathered = lax.all_gather(vec_low[row:], ("stream", "replica"), axis=0, tiled=True)
-    segmask = doc_segments[0][None, :] == jnp.arange(NSEG)[:, None]
+    slot_stream = my_stream ^ jnp.arange(streams)
+    slot_replica = my_replica ^ jnp.arange(replicas)
+    slot_device = (slot_stream[:, None] * replicas + slot_replica[None, :]).reshape(devices)
+
+    query_in = query_embeds.reshape(qtok, width)
+    query_tables = tables(jnp.arange(qtok, dtype=jnp.int32) // qlen)
+    query_vecs, query_kept = encode(query_in, *query_tables, mats, vectors)
+    query_low = query_vecs.astype(jnp.bfloat16)
+    all_query = spread(spread(query_low, "replica"), "stream")
+
+    doc_in = doc_embeds[0]
+    doc_tables = tables(doc_segments[0])
+    doc_vecs, doc_kept = encode(doc_in, *doc_tables, mats, vectors)
+    doc_low = doc_vecs.astype(jnp.bfloat16)
+    pdim = doc_low.shape[1]
+
+    tokens = devices * qtok
+    rows_all = all_query.reshape(tokens, pdim)
+    segment = doc_segments[0]
+    sims = (
+        lax.dot_general(
+            doc_low, rows_all, (((1,), (1,)), ((), ())), preferred_element_type=jnp.float32
+        )
+        / SOFT
+    )
+    weight = jnp.exp(sims)
+    segmask = (segment[None, :] == jnp.arange(NSEG)[:, None]).astype(jnp.float32)
+    totals = jnp.stack(
+        [jnp.sum(jnp.where((segment == d)[:, None], weight, 0.0), 0) for d in range(NSEG)], 0
+    )
+    scores = (SOFT * jnp.log(totals)).reshape(NSEG, devices, qdev, qlen).sum(-1)
+    scores = jnp.take(scores, slot_device, axis=1).reshape(NSEG, devices * qdev)
+    table = spread(spread(scores, "replica"), "stream").reshape(devices * NSEG, devices * qdev)
+    docs = (slot_device[:, None] * NSEG + jnp.arange(NSEG)[None, :]).reshape(-1)
+    slots = jnp.arange(candidates.shape[1])
+    named = (candidates[None] == docs[:, None, None]) & (slots <= neg_counts[:, None])[None]
+    first = (candidates[:, 0][None] == docs[:, None]).astype(jnp.float32)
+    listed = jnp.any(named, -1)
+    logits = jnp.where(listed, table, -1e30)
+    peak = jnp.max(logits, 0, keepdims=True)
+    expo = jnp.exp(logits - peak)
+    total = jnp.sum(expo, 0, keepdims=True)
     total_queries = candidates.shape[0]
-    my_docs = lax.axis_index(("stream", "replica")) * NSEG + jnp.arange(NSEG)
-    owned = (candidates[:, :, None] == my_docs[None, None, :]).astype(jnp.float32)
-    query_rows = gathered.reshape(total_queries, qlen, pdim)
-    chosen_count = query_rows.shape[0]
-    rows_all = chosen_count * qlen
-    block_rows = math.gcd(rows_all, 512)
-    blocks = query_rows.reshape(rows_all // block_rows, block_rows, pdim)
-
-    def sim_block(rows):
-        sim = jnp.dot(rows, doc_vecs.T, preferred_element_type=jnp.float32) / SOFT
-        return jnp.where(segmask[None], sim[:, None, :], -1e30)
-
-    def block_total(rows):
-        masked = sim_block(rows)
-        peak = jnp.max(masked, -1, keepdims=True)
-        return peak[..., 0] + jnp.log(jnp.sum(jnp.exp(masked - peak), -1))
-
-    log_total = lax.map(block_total, blocks)
-    chosen_scores = (SOFT * log_total).reshape(chosen_count, qlen, NSEG).sum(1)
-    table = lax.all_gather(chosen_scores, ("stream", "replica"), axis=1, tiled=True)
-    picked = jnp.take_along_axis(table, candidates, 1)
-    losses, grad_logits = cross_entropy(picked, neg_counts, total_queries)
+    losses = peak[0] + jnp.log(total[0]) - jnp.sum(table * first, 0)
     loss = jnp.mean(losses)
-    grad_scores = jnp.einsum("qc,qcs->qs", grad_logits, owned)
-    token_grads = jnp.repeat(grad_scores, qlen, axis=0).reshape(blocks.shape[0], block_rows, NSEG)
-
-    def back_block(doc_grad, items):
-        rows, totals, grads = items
-        weight = jnp.exp(sim_block(rows) - totals[..., None])
-        sim_low = jnp.einsum("bs,bsu->bu", grads, weight).astype(jnp.bfloat16)
-        return (
-            doc_grad + inner(sim_low, rows),
-            jnp.dot(sim_low, doc_vecs, preferred_element_type=jnp.float32),
-        )
-
-    doc_grad, query_grad = lax.scan(
-        back_block, jnp.zeros((row, pdim), jnp.float32), (blocks, log_total, token_grads)
-    )
-    query_grad = query_grad.reshape(chosen_count, qlen * pdim)
-    query_local = lax.psum_scatter(
-        query_grad.reshape(total_queries * qlen, pdim),
-        ("stream", "replica"),
-        scatter_dimension=0,
-        tiled=True,
-    )
-    grad_vec = jnp.concatenate([doc_grad, query_local], 0)
-    kept = encode(lax.optimization_barrier(tokens_in), same, cosine, sine, mats, vectors)[1]
-    grads = backward(grad_vec, tokens_in, cosine, sine, kept, mats, vectors)
-    grads = (
-        lax.psum(grads[0].astype(jnp.bfloat16), "stream").astype(jnp.float32),
-        lax.psum(grads[1].astype(jnp.bfloat16), "stream").astype(jnp.float32),
-        lax.psum(grads[2].astype(jnp.bfloat16), "stream").astype(jnp.float32),
-        lax.psum(grads[3].astype(jnp.bfloat16), "stream").astype(jnp.float32),
-        lax.psum(grads[4].astype(jnp.bfloat16), "stream").astype(jnp.float32),
-        lax.psum(grads[5].astype(jnp.bfloat16), "stream").astype(jnp.float32),
-    )
-    replicas = lax.axis_size("replica")
-    devices = lax.axis_size("stream") * replicas
-    rate = RATE * qdev * math.sqrt(devices / tokens_in.shape[0])
-    errs = (err_qkv, err_out, err_up, err_down, err_head)
-    facs = (fac_qkv, fac_out, fac_up, fac_down, fac_head)
-    moms = (mom_qkv, mom_out, mom_up, mom_down, mom_head)
-    merged = [grads[number] + errs[number][0] for number in range(5)]
-    lefts = [jnp.dot(merged[number], facs[number], precision=HIGH) for number in range(5)]
-    summed = lax.psum((lefts[0], lefts[1], lefts[2], lefts[3], lefts[4], grads[5]), "replica")
-    bases = [orthogonal(summed[number]) for number in range(5)]
-    rights_local = [
-        lax.dot_general(merged[number], bases[number], (((0,), (0,)), ((), ())), precision=HIGH)
-        for number in range(5)
+    grad_table = (expo / total - first) / total_queries
+    own = jnp.take(
+        grad_table[:NSEG].reshape(NSEG, devices, qdev), slot_device, axis=1
+    )
+    per_token = jnp.repeat(own.reshape(NSEG, devices * qdev), qlen, axis=1) / totals
+    spots = jnp.sum(segmask[:, :, None] * per_token[:, None, :], 0)
+    sim_low = (weight * spots).astype(jnp.bfloat16)
+    query_grad = lax.dot_general(
+        sim_low, doc_low, (((0,), (0,)), ((), ())), preferred_element_type=jnp.float32
+    ).reshape(streams, replicas, qtok, pdim)
+    query_local = fold(fold(query_grad, "stream"), "replica")
+    doc_grad = jnp.dot(sim_low, rows_all, preferred_element_type=jnp.float32)
+
+    doc_pairs, doc_packed = backward(doc_grad, doc_in, *doc_tables[1:], doc_kept, mats, vectors)
+    query_pairs, query_packed = backward(
+        query_local, query_in, *query_tables[1:], query_kept, mats, vectors
+    )
+    pairs = [
+        (jnp.concatenate([dx, qx], 0), jnp.concatenate([dy, qy], 0))
+        for (dx, dy), (qx, qy) in zip(doc_pairs, query_pairs)
     ]
-    rights = lax.psum(
-        (rights_local[0], rights_local[1], rights_local[2], rights_local[3], rights_local[4]),
-        "replica",
-    )
+    packed = doc_packed + query_packed
+    grads = [lax.psum(inner(x, y).astype(jnp.bfloat16), "stream") for x, y in pairs]
+
+    lefts = []
+    for (x, y), err, fac in zip(pairs, errs, facs):
+        tall = exact(fac.T, y, ((1,), (1,)))
+        left = exact(tall, x, ((1,), (0,)))
+        part = err.shape[0] // streams
+        rows = lax.dynamic_slice_in_dim(err, my_stream * part, part, 0)
+        mine = lax.dot_general(fac, rows, (((0,), (1,)), ((), ())), precision=HIGH)
+        keep = jnp.arange(err.shape[0]) // part == my_stream
+        left = left + jnp.where(keep[None], jnp.tile(mine, (1, streams)), 0.0)
+        lefts.append(left)
+    edges = [0]
+    for left in lefts:
+        edges.append(edges[-1] + left.shape[1])
+    bounds = list(zip(edges[:-1], edges[1:]))
+    summed = all_sum(jnp.concatenate(lefts, 1))
+    basis = pl.pallas_call(
+        lambda *refs: basis_kernel(bounds, *refs),
+        out_shape=jax.ShapeDtypeStruct(summed.shape, jnp.float32),
+        name="basis",
+    )(summed)
+    bases = [basis[:, lo:hi] for lo, hi in bounds]
+
+    rights = []
+    for (x, y), err, base in zip(pairs, errs, bases):
+        tall = exact(base, x, ((1,), (1,)))
+        right = exact(tall, y, ((1,), (0,)))
+        part = err.shape[0] // streams
+        rows = lax.dynamic_slice_in_dim(err, my_stream * part, part, 0)
+        share = lax.dynamic_slice_in_dim(base, my_stream * part, part, 1)
+        right = right + jnp.dot(share, rows, precision=HIGH)
+        rights.append(right)
+    edges = [0]
+    for right in rights:
+        edges.append(edges[-1] + right.shape[1])
+    side = -(-packed.shape[0] // 1024) * 128
+    packed = jnp.pad(packed, (0, 8 * side - packed.shape[0])).reshape(8, side)
+    joined = jnp.concatenate(rights + [packed], 1)
+    short = -joined.shape[1] % (128 * devices) if devices <= 32 else -joined.shape[1] % devices
+    joined = all_sum(jnp.pad(joined, ((0, 0), (0, short))))
+    rights = [joined[:, lo:hi] for lo, hi in zip(edges[:-1], edges[1:])]
+    packed_sum = joined[:, edges[-1] : edges[-1] + side].reshape(-1)[: vectors.shape[0]]
+
+    rate = RATE * qdev * math.sqrt(devices / (row + qtok))
     new_w, new_m, new_e = ([], [], [])
     for number in range(5):
-        approx = jnp.dot(bases[number], rights[number].T, precision=HIGH)
-        new_e.append((merged[number] - approx / replicas)[None])
+        approx = lax.dot_general(
+            bases[number], rights[number], (((0,), (0,)), ((), ())), precision=HIGH
+        )
+        merged = grads[number].astype(jnp.float32) + errs[number]
+        new_e.append((merged - approx / replicas)[None])
         momentum = MOMENTUM * moms[number] + approx
         new_m.append(momentum)
         new_w.append(weights[number] - rate * momentum)
-    vec_mom = MOMENTUM * mom_vectors + summed[5]
+    vec_mom = MOMENTUM * mom_vectors + packed_sum
     new_vec = vectors - rate * vec_mom
     return (
         loss,
-        new_w[0],
-        new_w[1],
-        new_w[2],
-        new_w[3],
-        new_w[4],
+        *new_w,
         new_vec,
-        new_m[0],
-        new_m[1],
-        new_m[2],
-        new_m[3],
-        new_m[4],
+        *new_m,
         vec_mom,
-        new_e[0],
-        new_e[1],
-        new_e[2],
-        new_e[3],
-        new_e[4],
-        rights[0],
-        rights[1],
-        rights[2],
-        rights[3],
-        rights[4],
+        *new_e,
+        *[right.T for right in rights],
     )
 
 

time: 1010 us -> 414 us (0.41)
  other arithmetic: 388 us -> 54.7 us
  waiting for transfers between devices: 207 us -> 64 us
  blocking collectives: 130 us -> 12.5 us
  starting transfers between devices: 0.33 us -> 49.8 us
  matrix products: 165 us -> 123 us
  between operations: 44.8 us -> 18.8 us
  local copies, waits for them, and re-layouts: 58 us -> 81 us
    reduce_sum x76 -> x5, other arithmetic: 228 us -> 2.54 us  [the longest x1 1.21 us: shards(): spots = jnp.sum(segmask[:, :, None] * per_token[:, None, :], 0)]
    mul x11 -> x2, other arithmetic: 98.8 us -> 0.01 us  [the longest x1 0.01 us: shards(): docs = (slot_device[:, None] * NSEG + jnp.arange(NSEG)[None, :]).reshape(-1)]
    unnamed x4 -> x1, waiting for transfers between devices: 94.5 us -> 0.02 us
    all_gather x2 -> x0, blocking collectives: 82.3 us -> none  [the longest x1 45.4 us: shards(): lax.all_gather(vec_low[row:], ('stream', 'replica'), axis=0, tiled=True)]
    psum x2 -> x1, waiting for transfers between devices: 112 us -> 38.4 us  [shards(): lax.psum(inner(x, y).astype(jnp.bfloat16), 'stream')]
    psum x2 -> x0, blocking collectives: 48.2 us -> none  [the longest x1 31.7 us: shards(): lax.psum((rights_local[0], rights_local[1], rights_local[2], rights_local...]
    ppermute x0 -> x30, starting transfers between devices: none -> 36.5 us  [the longest x20 24.8 us: spread(): lax.ppermute(value, axis, turn)]
    sub x1 -> x0, other arithmetic: 22.1 us -> none  [encode(): expo = jnp.exp(scores - jnp.max(scores, -1, keepdims=True))]
  transfers between devices with their start and end apart: 3 -> 34, of which waited for: 3 -> 9; matrix products, arithmetic and copies ran while one was open for 5% -> 34% of each run, Pallas kernels for 0% -> 1%
where the time goes in v1:
time: 414 us; the launch traced here: 407 us
  matrix products  123 us (30%)
  local copies, waits for them, and re-layouts  81 us (20%)
  waiting for transfers between devices  64 us (15%)
  other arithmetic  54.7 us (13%)
  starting transfers between devices  49.8 us (12%)
  between operations  18.8 us (5%)
  blocking collectives  12.5 us (3%)
    psum x1, waiting for transfers between devices, shards(): lax.psum(inner(x, y).astype(jnp.bfloat16), 'stream')  38.4 us
    unnamed x387, local copies, waits for them, and re-layouts  28.7 us
    dot_general x5, matrix products, shards(): lax.dot_general(bases[number], rights[number], (((0,), (0,)), ((), ())),...  26 us
    ppermute x20, starting transfers between devices, spread(): lax.ppermute(value, axis, turn)  24.8 us
    all_to_all x1, blocking collectives, all_sum(): got = lax.all_to_all(pieces, axes, 0, 0, tiled=True)  12.5 us
    ppermute x10, starting transfers between devices, fold(): total = total + lax.ppermute(value[k], axis, turn)  11.6 us
    dot_general x5, matrix products, inner(): lax.dot_general(first, second, (((0,), (0,)), ((), ())), preferred_elemen...  11.5 us
    all_to_all x2, waiting for transfers between devices, all_sum(): lax.all_to_all(jnp.broadcast_to(mine[None], pieces.shape), axes, 0, 0, ti...  11.5 us
  transfers between devices with their start and end apart: 34, of which 9 were waited for; matrix products, arithmetic and copies ran while one was open for 34% of the time, Pallas kernels for 1%

profile of v1, /device:TPU:0, one launch (start us, length us, event | category | flops | bytes accessed | tf_op | source)
XLA Modules:
  0.0 406.8 jit_solution(17744612121254971673)
XLA Ops:
  19.1 2.0 copy.227
  24.1 1.9 fusion.344
  33.5 2.6 collective-permute-start.1
  36.2 2.8 collective-permute-start.3
  41.3 2.2 convolution_add_fusion
  43.5 3.5 copy.225
  50.7 8.2 %fusion.347 = (f32[12,512]{1,0:T(8,128)S(1)}, f32[12,512,512]{1,2,0:T(8,128)}) fusion(pred[512,512]{0,1:T(8,128)(4,1)} %broadcast_compare_fusion, bf16[512,12,32]{0,2,1:T(8,128)(2,1)S(1)} %get-tuple-element.98, bf16[512,12,32]{0,2,1:T(8,128)(2,1)S(1)} %get-tuple-element.97), kind=kOutput, calls=%fused_computation.732 | convolution fusion | flops 213910016 | bytes 13656064 | tf_op jit(solution)/shard_map/sub | solution.py:101
  59.5 6.0 %fusion.29 = bf16[12,32,512]{2,1,0:T(8,128)(2,1)S(1)} fusion(f32[512,3,12,32]{0,3,2,1:T(8,128)} %bitcast.346, f32[12,512,512]{1,2,0:T(8,128)} %get-tuple-element.247, f32[12,512]{1,0:T(8,128)S(1)} %get-tuple-element.246), kind=kOutput, calls=%fused_computation.72 | convolution fusion | flops 207814656 | bytes 13393920 | tf_op jit(solution)/shard_map/hij,jhd->ihd/dot_general | solution.py:105
  67.0 2.5 multiply_convert_fusion.2
  78.1 2.1 convolution_bitcast_fusion.9
  82.0 2.2 convolution_bitcast_fusion.7
  85.9 2.3 convolution_bitcast_fusion.5
  89.5 3.5 collective-permute-start.5
  105.2 3.9 collective-permute-done.7
  109.1 4.7 %collective-permute-done.8 = bf16[8,64,96]{1,2,0:T(8,128)(2,1)S(1)} collective-permute-done((bf16[8,64,96]{1,2,0:T(8,128)(2,1)}, bf16[8,64,96]{1,2,0:T(8,128)(2,1)S(1)}, u32[]{:S(2)}, u32[]{:S(2)}) %collective-permute-start.8) | collective-permute-done | bytes 98336 | tf_op jit(solution)/shard_map/ppermute | solution.py:232
  113.9 2.0 pad_maximum_fusion.4
  115.9 2.2 copy.230
  118.1 5.0 %select_reduce_fusion.3 = (f32[2048]{0:T(1024)S(1)}, f32[2048]{0:T(1024)S(1)}, f32[2048]{0:T(1024)S(1)}, f32[2048]{0:T(1024)S(1)}, f32[512,2048]{1,0:T(8,128)}) fusion(pred[512]{0:T(512)(128)(4,1)S(1)} %copy-done.173, pred[512]{0:T(512)(128)(4,1)S(1)} %copy-done.171, pred[512]{0:T(512)(128)(4,1)S(1)} %copy-done.172, pred[512]{0:T(512)(128)(4,1)S(1)} %copy-done.170, ...), kind=kOutput, calls=%fused_computation.19 | convolution fusion | flops 210853888 | bytes 4820992 | tf_op jit(solution)/shard_map/dot_general | solution.py:348
  127.1 1.8 collective-permute-start.12
  128.9 2.4 collective-permute-start.13
  131.5 3.5 collective-permute-start.15
  169.3 6.9 %multiply_reduce_fusion.1 = (f32[12,512]{1,0:T(8,128)S(1)}, f32[12,512,512]{1,2,0:T(8,128)}) fusion(f32[12,512,512]{1,2,0:T(8,128)S(1)} %bitcast.350, f32[12,512]{1,0:T(8,128)S(1)} %copy-done.118, bf16[512,12,32]{0,2,1:T(8,128)(2,1)S(1)} %bitcast.373, f32[512,3,12,32]{0,3,2,1:T(8,128)} %bitcast.347), kind=kOutput, calls=%fused_computation.6 | convolution fusion | flops 210757632 | bytes 26001408 | tf_op jit(solution)/shard_map/ihd,jhd->hij/dot_general | solution.py:186
  176.3 2.9 fusion.26
  187.5 10.1 %multiply_convert_fusion = bf16[12,512,512]{1,2,0:T(8,128)(2,1)S(1)} fusion(f32[12,512,512]{1,2,0:T(8,128)} %get-tuple-element.269, f32[12,512]{1,0:T(8,128)S(1)} %get-tuple-element.268, f32[12,512,512]{1,2,0:T(8,128)} %get-tuple-element.247, f32[12,512]{1,0:T(8,128)S(1)} %copy-done.118), kind=kLoop, calls=%fused_computation.5 | loop fusion | flops 12582912 | bytes 31506432 | tf_op jit(solution)/shard_map/convert_element_type | solution.py:193
  197.6 1.9 convolution_bitcast_fusion
  203.9 1.9 copy.253
  205.8 2.7 fusion.21
  210.2 1.8 collective-permute-start.25
  214.7 2.1 collective-permute-start.28
  235.1 2.0 fusion.58
  238.1 1.9 convolution_convert_fusion.2
  242.7 4.0 all-to-all-start
  257.1 3.8 convolution_convert_fusion.1
  261.6 5.8 %all-to-all-start.1 = ((f32[32,8,96]{2,1,0:T(8,128)}), f32[32,8,96]{2,1,0:T(8,128)S(1)}, u32[]{:S(2)}, u32[]{:S(2)}) async-start(f32[32,8,96]{2,1,0:T(8,128)} %broadcast_in_dim.134), calls=%async_computation.1 | async-start | bytes 262144 | tf_op jit(solution)/shard_map/all_to_all | solution.py:251
  268.4 3.8 convolution_convert_fusion
  272.2 3.4 all-to-all-done.1
  276.4 3.1 basis.1
  282.4 2.0 fusion.55
  292.4 2.1 convolution_add_fusion.5
  297.0 12.5 %all_to_all.20 = f32[32,8,256]{2,1,0:T(8,128)} all-to-all(f32[32,8,256]{2,1,0:T(8,128)S(1)} %bitcast.367), channel_id=1, replica_groups=mesh['stream'=4,'replica'=8] {'stream','replica'}, dimensions={0} | all-to-all | bytes 524288 | tf_op jit(solution)/shard_map/all_to_all | solution.py:249
  311.2 3.3 all-to-all-start.3
  316.5 8.0 %all-to-all-done.3 = f32[32,8,256]{2,1,0:T(8,128)} async-done(((f32[32,8,256]{2,1,0:T(8,128)}), f32[32,8,256]{2,1,0:T(8,128)}, u32[]{:S(2)}, u32[]{:S(2)}) %all-to-all-start.3) | async-done | bytes 262176 | tf_op jit(solution)/shard_map/all_to_all | solution.py:251
  334.1 38.4 %all-reduce.5.cloned.1.call-done = (bf16[384,1152]{1,0:T(8,128)(2,1)}, bf16[384,384]{1,0:T(8,128)(2,1)}, bf16[384,1536]{1,0:T(8,128)(2,1)}, bf16[1536,384]{1,0:T(8,128)(2,1)}, bf16[384,96]{0,1:T(8,128)(2,1)}) async-done(((bf16[384,1152]{1,0:T(8,128)(2,1)}, bf16[384,384]{1,0:T(8,128)(2,1)}, bf16[384,1536]{1,0:T(8,128)(2,1)}, bf16[1536,384]{1,0:T(8,128)(2,1)}, bf16[384,96]{0,1:T(8,128)(2,1)}), ...) | async-done | bytes 3612688 | tf_op jit(solution)/shard_map/psum | solution.py:395
  372.5 2.2 multiply_subtract_fusion.4
  374.7 9.1 %multiply_subtract_fusion = (f32[1536,384]{1,0:T(8,128)}, f32[1536,384]{1,0:T(8,128)}, f32[1,1536,384]{2,1,0:T(8,128)}) fusion(f32[1536,384]{1,0:T(8,128)} %param.37, f32[1536,384]{1,0:T(8,128)} %param.43, f32[1,1536,384]{2,1,0:T(8,128)} %param.49, bf16[1536,384]{1,0:T(8,128)(2,1)} %get-tuple-element.47, f32[8,8192]{1,0:T(8,128)} %bitcast.103, ...), kind=kOutput, calls=%fused_computation.45 | convolution fusion | flops 61341696 | bytes 15396864 | tf_op jit(solution)/shard_map/dot_general | solution.py:442
  383.9 6.6 %multiply_subtract_fusion.1 = (f32[384,1536]{1,0:T(8,128)}, f32[384,1536]{1,0:T(8,128)}, f32[1,384,1536]{2,1,0:T(8,128)}) fusion(f32[384,1536]{1,0:T(8,128)S(1)} %copy-done.7, f32[384,1536]{1,0:T(8,128)S(1)} %copy-done.19, f32[1,384,1536]{2,1,0:T(8,128)S(1)} %copy-done.11, bf16[384,1536]{1,0:T(8,128)(2,1)S(1)} %copy-done.36, f32[8,8192]{1,0:T(8,128)} %bitcast.103, ...), kind=kOutput, calls=%fused_computation.47 | convolution fusion | flops 61341696 | bytes 15396864 | tf_op jit(solution)/shard_map/dot_general | solution.py:442
  390.5 2.9 multiply_subtract_fusion.3
  393.5 5.1 %multiply_subtract_fusion.2 = (f32[384,1152]{1,0:T(8,128)}, f32[384,1152]{1,0:T(8,128)}, f32[1,384,1152]{2,1,0:T(8,128)}) fusion(f32[384,1152]{1,0:T(8,128)S(1)} %copy-done, f32[384,1152]{1,0:T(8,128)S(1)} %copy-done.22, f32[1,384,1152]{2,1,0:T(8,128)S(1)} %copy-done.17, bf16[384,1152]{1,0:T(8,128)(2,1)S(1)} %copy-done.39, f32[8,8192]{1,0:T(8,128)} %bitcast.103, ...), kind=kOutput, calls=%fused_computation.58 | convolution fusion | flops 46006272 | bytes 11550720 | tf_op jit(solution)/shard_map/dot_general | solution.py:442
  (695 shorter events, 170.0 us)
Async XLA Ops:
  9.5 22.1 %copy-start.124 = (f32[384]{0:T(512)}, f32[384]{0:T(512)S(1)}, u32[]{:S(2)}) copy-start(f32[384]{0:T(512)S(1)} %get-tuple-element.202) | copy-start | bytes 4612
  33.0 56.5 %collective-permute-start = (bf16[64,96]{0,1:T(8,128)(2,1)}, bf16[64,96]{0,1:T(8,128)(2,1)}, u32[]{:S(2)}, u32[]{:S(2)}) collective-permute-start(bf16[64,96]{0,1:T(8,128)(2,1)} %get-tuple-element.94), channel_id=1, source_target_pairs={{0,1},{1,0},{2,3},{3,2},{4,5},{5,4},{6,7},{7,6},{8,9},{9,8},{10,11... | collective-permute-start | bytes 36872 | tf_op jit(solution)/shard_map/ppermute | solution.py:232
  33.5 60.8 %collective-permute-start.1 = (bf16[64,96]{0,1:T(8,128)(2,1)}, bf16[64,96]{0,1:T(8,128)(2,1)}, u32[]{:S(2)}, u32[]{:S(2)}) collective-permute-start(bf16[64,96]{0,1:T(8,128)(2,1)} %get-tuple-element.94), channel_id=1, source_target_pairs={{0,2},{1,3},{2,0},{3,1},{4,6},{5,7},{6,4},{7,5},{8,10},{9,11},{10,... | collective-permute-start | bytes 36872 | tf_op jit(solution)/shard_map/ppermute | solution.py:232
  36.1 59.8 %collective-permute-start.2 = (bf16[64,96]{0,1:T(8,128)(2,1)}, bf16[64,96]{0,1:T(8,128)(2,1)}, u32[]{:S(2)}, u32[]{:S(2)}) collective-permute-start(bf16[64,96]{0,1:T(8,128)(2,1)} %get-tuple-element.94), channel_id=1, source_target_pairs={{0,3},{1,2},{2,1},{3,0},{4,7},{5,6},{6,5},{7,4},{8,11},{9,10},{10,... | collective-permute-start | bytes 36872 | tf_op jit(solution)/shard_map/ppermute | solution.py:232
  36.2 61.0 %collective-permute-start.3 = (bf16[64,96]{0,1:T(8,128)(2,1)}, bf16[64,96]{0,1:T(8,128)(2,1)}, u32[]{:S(2)}, u32[]{:S(2)}) collective-permute-start(bf16[64,96]{0,1:T(8,128)(2,1)} %get-tuple-element.94), channel_id=1, source_target_pairs={{0,4},{1,5},{2,6},{3,7},{4,0},{5,1},{6,2},{7,3},{8,12},{9,13},{10,... | collective-permute-start | bytes 36872 | tf_op jit(solution)/shard_map/ppermute | solution.py:232
  39.0 59.6 %collective-permute-start.4 = (bf16[64,96]{0,1:T(8,128)(2,1)}, bf16[64,96]{0,1:T(8,128)(2,1)}, u32[]{:S(2)}, u32[]{:S(2)}) collective-permute-start(bf16[64,96]{0,1:T(8,128)(2,1)} %get-tuple-element.94), channel_id=1, source_target_pairs={{0,5},{1,4},{2,7},{3,6},{4,1},{5,0},{6,3},{7,2},{8,13},{9,12},{10,... | collective-permute-start | bytes 36872 | tf_op jit(solution)/shard_map/ppermute | solution.py:232
  70.8 17.5 %copy-start.105 = (f32[512]{0:T(512)}, f32[512]{0:T(512)S(1)}, u32[]{:S(2)}) copy-start(f32[512]{0:T(512)S(1)} %broadcast_multiply_fusion.13) | copy-start | bytes 6148
  72.8 45.3 %copy-start.115 = (f32[512]{0:T(512)}, f32[512]{0:T(512)S(1)}, u32[]{:S(2)}) copy-start(f32[512]{0:T(512)S(1)} %add_rsqrt_fusion) | copy-start | bytes 6148
  82.0 36.1 %copy-start.170 = (pred[512]{0:T(512)(128)(4,1)S(1)}, pred[512]{0:T(512)(128)(4,1)}, u32[]{:S(2)}) copy-start(pred[512]{0:T(512)(128)(4,1)} %get-tuple-element.226) | copy-start | bytes 1540
  82.0 36.1 %copy-start.171 = (pred[512]{0:T(512)(128)(4,1)S(1)}, pred[512]{0:T(512)(128)(4,1)}, u32[]{:S(2)}) copy-start(pred[512]{0:T(512)(128)(4,1)} %get-tuple-element.227) | copy-start | bytes 1540
  82.0 36.1 %copy-start.172 = (pred[512]{0:T(512)(128)(4,1)S(1)}, pred[512]{0:T(512)(128)(4,1)}, u32[]{:S(2)}) copy-start(pred[512]{0:T(512)(128)(4,1)} %get-tuple-element.228) | copy-start | bytes 1540
  82.0 36.1 %copy-start.173 = (pred[512]{0:T(512)(128)(4,1)S(1)}, pred[512]{0:T(512)(128)(4,1)}, u32[]{:S(2)}) copy-start(pred[512]{0:T(512)(128)(4,1)} %get-tuple-element.229) | copy-start | bytes 1540
  89.5 10.4 %collective-permute-start.5 = (bf16[64,96]{0,1:T(8,128)(2,1)}, bf16[64,96]{0,1:T(8,128)(2,1)S(1)}, u32[]{:S(2)}, u32[]{:S(2)}) collective-permute-start(bf16[64,96]{0,1:T(8,128)(2,1)} %get-tuple-element.94), channel_id=1, source_target_pairs={{0,6},{1,7},{2,4},{3,5},{4,2},{5,3},{6,0},{7,1},{8,14},{9,15},{10,... | collective-permute-start | bytes 36872 | tf_op jit(solution)/shard_map/ppermute | solution.py:232
  94.4 6.1 %collective-permute-start.6 = (bf16[64,96]{0,1:T(8,128)(2,1)}, bf16[64,96]{0,1:T(8,128)(2,1)S(1)}, u32[]{:S(2)}, u32[]{:S(2)}) collective-permute-start(bf16[64,96]{0,1:T(8,128)(2,1)} %get-tuple-element.94), channel_id=1, source_target_pairs={{0,7},{1,6},{2,5},{3,4},{4,3},{5,2},{6,1},{7,0},{8,15},{9,14},{10,... | collective-permute-start | bytes 36872 | tf_op jit(solution)/shard_map/ppermute | solution.py:232
  101.1 8.0 %collective-permute-start.7 = (bf16[8,64,96]{1,2,0:T(8,128)(2,1)}, bf16[8,64,96]{1,2,0:T(8,128)(2,1)S(1)}, u32[]{:S(2)}, u32[]{:S(2)}) collective-permute-start(bf16[8,64,96]{1,2,0:T(8,128)(2,1)} %constant_dynamic-update-slice_fusion), channel_id=1, source_target_pairs={{0,8},{8,0},{16,24},{24,16},{1,9},{9,1},{17,25},{25,17},{2,10},{10... | collective-permute-start | bytes 294920 | tf_op jit(solution)/shard_map/ppermute | solution.py:232
  102.6 11.2 %collective-permute-start.8 = (bf16[8,64,96]{1,2,0:T(8,128)(2,1)}, bf16[8,64,96]{1,2,0:T(8,128)(2,1)S(1)}, u32[]{:S(2)}, u32[]{:S(2)}) collective-permute-start(bf16[8,64,96]{1,2,0:T(8,128)(2,1)} %constant_dynamic-update-slice_fusion), channel_id=1, source_target_pairs={{0,16},{8,24},{16,0},{24,8},{1,17},{9,25},{17,1},{25,9},{2,18},{10... | collective-permute-start | bytes 294920 | tf_op jit(solution)/shard_map/ppermute | solution.py:232
  104.1 9.8 %collective-permute-start.9 = (bf16[8,64,96]{1,2,0:T(8,128)(2,1)}, bf16[8,64,96]{1,2,0:T(8,128)(2,1)S(1)}, u32[]{:S(2)}, u32[]{:S(2)}) collective-permute-start(bf16[8,64,96]{1,2,0:T(8,128)(2,1)} %constant_dynamic-update-slice_fusion), channel_id=1, source_target_pairs={{0,24},{8,16},{16,8},{24,0},{1,25},{9,17},{17,9},{25,1},{2,26},{10... | collective-permute-start | bytes 294920 | tf_op jit(solution)/shard_map/ppermute | solution.py:232
  123.2 34.1 %copy-start.107 = (f32[4,512]{1,0:T(4,128)S(1)}, f32[4,512]{1,0:T(4,128)}, u32[]{:S(2)}) copy-start(f32[4,512]{1,0:T(4,128)} %fusion.264) | copy-start | bytes 24580
  125.8 5.7 %collective-permute-start.10 = (f32[4,64]{0,1:T(8,128)S(1)}, f32[4,64]{0,1:T(8,128)S(1)}, u32[]{:S(2)}, u32[]{:S(2)}) collective-permute-start(f32[4,64]{0,1:T(8,128)S(1)} %bitcast.390), channel_id=1, source_target_pairs={{0,1},{1,0},{2,3},{3,2},{4,5},{5,4},{6,7},{7,6},{8,9},{9,8},{10,11... | collective-permute-start | bytes 3080 | tf_op jit(solution)/shard_map/ppermute | solution.py:232
  125.9 9.1 %collective-permute-start.11 = (f32[4,64]{0,1:T(8,128)S(1)}, f32[4,64]{0,1:T(8,128)S(1)}, u32[]{:S(2)}, u32[]{:S(2)}) collective-permute-start(f32[4,64]{0,1:T(8,128)S(1)} %bitcast.391), channel_id=1, source_target_pairs={{0,2},{1,3},{2,0},{3,1},{4,6},{5,7},{6,4},{7,5},{8,10},{9,11},{10,... | collective-permute-start | bytes 3080 | tf_op jit(solution)/shard_map/ppermute | solution.py:232
  127.1 10.1 %collective-permute-start.12 = (f32[4,64]{0,1:T(8,128)S(1)}, f32[4,64]{0,1:T(8,128)}, u32[]{:S(2)}, u32[]{:S(2)}) collective-permute-start(f32[4,64]{0,1:T(8,128)S(1)} %bitcast.392), channel_id=1, source_target_pairs={{0,3},{1,2},{2,1},{3,0},{4,7},{5,6},{6,5},{7,4},{8,11},{9,10},{10,... | collective-permute-start | bytes 3080 | tf_op jit(solution)/shard_map/ppermute | solution.py:232
  128.9 9.1 %collective-permute-start.13 = (f32[4,64]{0,1:T(8,128)S(1)}, f32[4,64]{0,1:T(8,128)S(1)}, u32[]{:S(2)}, u32[]{:S(2)}) collective-permute-start(f32[4,64]{0,1:T(8,128)S(1)} %bitcast.393), channel_id=1, source_target_pairs={{0,4},{1,5},{2,6},{3,7},{4,0},{5,1},{6,2},{7,3},{8,12},{9,13},{10,... | collective-permute-start | bytes 3080 | tf_op jit(solution)/shard_map/ppermute | solution.py:232
  131.3 6.7 %collective-permute-start.14 = (f32[4,64]{0,1:T(8,128)S(1)}, f32[4,64]{0,1:T(8,128)S(1)}, u32[]{:S(2)}, u32[]{:S(2)}) collective-permute-start(f32[4,64]{0,1:T(8,128)S(1)} %bitcast.394), channel_id=1, source_target_pairs={{0,5},{1,4},{2,7},{3,6},{4,1},{5,0},{6,3},{7,2},{8,13},{9,12},{10,... | collective-permute-start | bytes 3080 | tf_op jit(solution)/shard_map/ppermute | solution.py:232
  131.5 6.6 %collective-permute-start.15 = (f32[4,64]{0,1:T(8,128)S(1)}, f32[4,64]{0,1:T(8,128)}, u32[]{:S(2)}, u32[]{:S(2)}) collective-permute-start(f32[4,64]{0,1:T(8,128)S(1)} %bitcast.395), channel_id=1, source_target_pairs={{0,6},{1,7},{2,4},{3,5},{4,2},{5,3},{6,0},{7,1},{8,14},{9,15},{10,... | collective-permute-start | bytes 3080 | tf_op jit(solution)/shard_map/ppermute | solution.py:232
  135.0 5.3 %collective-permute-start.16 = (f32[4,64]{0,1:T(8,128)S(1)}, f32[4,64]{0,1:T(8,128)}, u32[]{:S(2)}, u32[]{:S(2)}) collective-permute-start(f32[4,64]{0,1:T(8,128)S(1)} %bitcast.396), channel_id=1, source_target_pairs={{0,7},{1,6},{2,5},{3,4},{4,3},{5,2},{6,1},{7,0},{8,15},{9,14},{10,... | collective-permute-start | bytes 3080 | tf_op jit(solution)/shard_map/ppermute | solution.py:232
  141.9 9.5 %collective-permute-start.17 = (f32[8,4,64]{2,0,1:T(8,128)S(1)}, f32[8,4,64]{2,0,1:T(8,128)S(1)}, u32[]{:S(2)}, u32[]{:S(2)}) collective-permute-start(f32[8,4,64]{2,0,1:T(8,128)S(1)} %stack.158), channel_id=1, source_target_pairs={{0,8},{8,0},{16,24},{24,16},{1,9},{9,1},{17,25},{25,17},{2,10},{10... | collective-permute-start | bytes 24584 | tf_op jit(solution)/shard_map/ppermute | solution.py:232
  143.1 8.3 %collective-permute-start.18 = (f32[8,4,64]{2,0,1:T(8,128)S(1)}, f32[8,4,64]{2,0,1:T(8,128)S(1)}, u32[]{:S(2)}, u32[]{:S(2)}) collective-permute-start(f32[8,4,64]{2,0,1:T(8,128)S(1)} %stack.158), channel_id=1, source_target_pairs={{0,16},{8,24},{16,0},{24,8},{1,17},{9,25},{17,1},{25,9},{2,18},{10... | collective-permute-start | bytes 24584 | tf_op jit(solution)/shard_map/ppermute | solution.py:232
  144.0 7.4 %collective-permute-start.19 = (f32[8,4,64]{2,0,1:T(8,128)S(1)}, f32[8,4,64]{2,0,1:T(8,128)S(1)}, u32[]{:S(2)}, u32[]{:S(2)}) collective-permute-start(f32[8,4,64]{2,0,1:T(8,128)S(1)} %stack.158), channel_id=1, source_target_pairs={{0,24},{8,16},{16,8},{24,0},{1,25},{9,17},{17,9},{25,1},{2,26},{10... | collective-permute-start | bytes 24584 | tf_op jit(solution)/shard_map/ppermute | solution.py:232
  181.9 26.6 %collective-permute-start.20 = (f32[8,64,96]{1,2,0:T(8,128)}, f32[8,64,96]{1,2,0:T(8,128)}, u32[]{:S(2)}, u32[]{:S(2)}) collective-permute-start(f32[8,64,96]{1,2,0:T(8,128)} %copy.252), channel_id=1, source_target_pairs={{0,8},{8,0},{16,24},{24,16},{1,9},{9,1},{17,25},{25,17},{2,10},{10... | collective-permute-start | bytes 589832 | tf_op jit(solution)/shard_map/ppermute | solution.py:240
  184.1 24.4 %collective-permute-start.21 = (f32[8,64,96]{1,2,0:T(8,128)}, f32[8,64,96]{1,2,0:T(8,128)}, u32[]{:S(2)}, u32[]{:S(2)}) collective-permute-start(f32[8,64,96]{1,2,0:T(8,128)} %copy.255), channel_id=1, source_target_pairs={{0,16},{8,24},{16,0},{24,8},{1,17},{9,25},{17,1},{25,9},{2,18},{10... | collective-permute-start | bytes 589832 | tf_op jit(solution)/shard_map/ppermute | solution.py:240
  186.0 22.5 %collective-permute-start.22 = (f32[8,64,96]{1,2,0:T(8,128)}, f32[8,64,96]{1,2,0:T(8,128)}, u32[]{:S(2)}, u32[]{:S(2)}) collective-permute-start(f32[8,64,96]{1,2,0:T(8,128)} %copy.257), channel_id=1, source_target_pairs={{0,24},{8,16},{16,8},{24,0},{1,25},{9,17},{17,9},{25,1},{2,26},{10... | collective-permute-start | bytes 589832 | tf_op jit(solution)/shard_map/ppermute | solution.py:240
  205.8 16.6 %copy-start.161 = (f32[64]{0:T(128)S(1)}, f32[64]{0:T(128)}, u32[]{:S(2)}) copy-start(f32[64]{0:T(128)} %copy-done.160) | copy-start | bytes 772
  208.5 16.2 %copy-start.15 = (bf16[1536,384]{1,0:T(8,128)(2,1)S(1)}, bf16[1536,384]{1,0:T(8,128)(2,1)}, u32[]{:S(2)}) copy-start(bf16[1536,384]{1,0:T(8,128)(2,1)} %convert_element_type.416) | copy-start | bytes 3538948
  208.5 16.2 %copy-start.47 = (f32[64,1536]{1,0:T(8,128)S(1)}, f32[64,1536]{1,0:T(8,128)}, u32[]{:S(2)}) copy-start(f32[64,1536]{1,0:T(8,128)} %get-tuple-element.241) | copy-start | bytes 1179652
  210.0 15.8 %copy-start.5 = (bf16[384,1536]{1,0:T(8,128)(2,1)S(1)}, bf16[384,1536]{1,0:T(8,128)(2,1)}, u32[]{:S(2)}) copy-start(bf16[384,1536]{1,0:T(8,128)(2,1)} %copy-done.2) | copy-start | bytes 3538948
  210.0 4.6 %collective-permute-start.23 = (f32[64,96]{0,1:T(8,128)S(1)}, f32[64,96]{0,1:T(8,128)S(1)}, u32[]{:S(2)}, u32[]{:S(2)}) collective-permute-start(f32[64,96]{0,1:T(8,128)S(1)} %get-tuple-element.125), channel_id=1, source_target_pairs={{0,1},{1,0},{2,3},{3,2},{4,5},{5,4},{6,7},{7,6},{8,9},{9,8},{10,11... | collective-permute-start | bytes 73736 | tf_op jit(solution)/shard_map/ppermute | solution.py:240
  210.1 6.7 %collective-permute-start.24 = (f32[64,96]{0,1:T(8,128)S(1)}, f32[64,96]{0,1:T(8,128)S(1)}, u32[]{:S(2)}, u32[]{:S(2)}) collective-permute-start(f32[64,96]{0,1:T(8,128)S(1)} %get-tuple-element.131), channel_id=1, source_target_pairs={{0,2},{1,3},{2,0},{3,1},{4,6},{5,7},{6,4},{7,5},{8,10},{9,11},{10,... | collective-permute-start | bytes 73736 | tf_op jit(solution)/shard_map/ppermute | solution.py:240
  210.2 8.0 %collective-permute-start.25 = (f32[64,96]{0,1:T(8,128)S(1)}, f32[64,96]{0,1:T(8,128)S(1)}, u32[]{:S(2)}, u32[]{:S(2)}) collective-permute-start(f32[64,96]{0,1:T(8,128)S(1)} %get-tuple-element.130), channel_id=1, source_target_pairs={{0,3},{1,2},{2,1},{3,0},{4,7},{5,6},{6,5},{7,4},{8,11},{9,10},{10,... | collective-permute-start | bytes 73736 | tf_op jit(solution)/shard_map/ppermute | solution.py:240
  212.0 7.4 %collective-permute-start.26 = (f32[64,96]{0,1:T(8,128)S(1)}, f32[64,96]{0,1:T(8,128)S(1)}, u32[]{:S(2)}, u32[]{:S(2)}) collective-permute-start(f32[64,96]{0,1:T(8,128)S(1)} %get-tuple-element.129), channel_id=1, source_target_pairs={{0,4},{1,5},{2,6},{3,7},{4,0},{5,1},{6,2},{7,3},{8,12},{9,13},{10,... | collective-permute-start | bytes 73736 | tf_op jit(solution)/shard_map/ppermute | solution.py:240
  213.1 7.7 %collective-permute-start.27 = (f32[64,96]{0,1:T(8,128)S(1)}, f32[64,96]{0,1:T(8,128)S(1)}, u32[]{:S(2)}, u32[]{:S(2)}) collective-permute-start(f32[64,96]{0,1:T(8,128)S(1)} %get-tuple-element.128), channel_id=1, source_target_pairs={{0,5},{1,4},{2,7},{3,6},{4,1},{5,0},{6,3},{7,2},{8,13},{9,12},{10,... | collective-permute-start | bytes 73736 | tf_op jit(solution)/shard_map/ppermute | solution.py:240
  214.7 6.1 %collective-permute-start.28 = (f32[64,96]{0,1:T(8,128)S(1)}, f32[64,96]{0,1:T(8,128)S(1)}, u32[]{:S(2)}, u32[]{:S(2)}) collective-permute-start(f32[64,96]{0,1:T(8,128)S(1)} %get-tuple-element.127), channel_id=1, source_target_pairs={{0,6},{1,7},{2,4},{3,5},{4,2},{5,3},{6,0},{7,1},{8,14},{9,15},{10,... | collective-permute-start | bytes 73736 | tf_op jit(solution)/shard_map/ppermute | solution.py:240
  216.8 5.6 %collective-permute-start.29 = (f32[64,96]{0,1:T(8,128)S(1)}, f32[64,96]{0,1:T(8,128)S(1)}, u32[]{:S(2)}, u32[]{:S(2)}) collective-permute-start(f32[64,96]{0,1:T(8,128)S(1)} %get-tuple-element.126), channel_id=1, source_target_pairs={{0,7},{1,6},{2,5},{3,4},{4,3},{5,2},{6,1},{7,0},{8,15},{9,14},{10,... | collective-permute-start | bytes 73736 | tf_op jit(solution)/shard_map/ppermute | solution.py:240
  242.7 18.2 %all-to-all-start = ((f32[32,8,96]{2,1,0:T(8,128)}), f32[32,8,96]{2,1,0:T(8,128)S(1)}, u32[]{:S(2)}, u32[]{:S(2)}) async-start(f32[32,8,96]{2,1,0:T(8,128)} %bitcast.343), calls=%async_computation | async-start | bytes 262144 | tf_op jit(solution)/shard_map/all_to_all | solution.py:249
  246.7 21.0 %copy-start.167 = (f32[96]{0:T(128)S(1)}, f32[96]{0:T(128)}, u32[]{:S(2)}) copy-start(f32[96]{0:T(128)} %get-tuple-element.143) | copy-start | bytes 1156
  246.7 21.0 %copy-start.123 = (f32[5088]{0:T(1024)S(1)}, f32[5088]{0:T(1024)}, u32[]{:S(2)}) copy-start(f32[5088]{0:T(1024)} %copy-done.122) | copy-start | bytes 61060
  261.6 14.0 %all-to-all-start.1 = ((f32[32,8,96]{2,1,0:T(8,128)}), f32[32,8,96]{2,1,0:T(8,128)S(1)}, u32[]{:S(2)}, u32[]{:S(2)}) async-start(f32[32,8,96]{2,1,0:T(8,128)} %broadcast_in_dim.134), calls=%async_computation.1 | async-start | bytes 262144 | tf_op jit(solution)/shard_map/all_to_all | solution.py:251
  267.5 105.0 %all-reduce.5.cloned.1.call-start = ((), (), s32[]{:S(2)}) async-start(), calls=%async_computation.4 | async-start | bytes 7225344 | tf_op jit(solution)/shard_map/psum | solution.py:395
  311.2 13.3 %all-to-all-start.3 = ((f32[32,8,256]{2,1,0:T(8,128)}), f32[32,8,256]{2,1,0:T(8,128)}, u32[]{:S(2)}, u32[]{:S(2)}) async-start(f32[32,8,256]{2,1,0:T(8,128)} %broadcast_in_dim.135), calls=%async_computation.3 | async-start | bytes 524288 | tf_op jit(solution)/shard_map/all_to_all | solution.py:251
  (168 other events, 710.1 us)
Sparse Core Ops, SparseCore 0:
  273.1 99.2 all-reduce.4
